TPU v7x, 32 devices: a whole 2x2x4 slice. The times are simulated.
32 devices in a mesh: grp: 4 (over x, core), uly: 8 (over z, y).
Axes of the slice: x: 2, y: 2, z: 4, core: 2. Of those that a mesh axis runs over, the one named last changes fastest.
Arguments:
- queries: bfloat16 [4096, 8192], P(('grp', 'uly')), may hold values from -6 to 6
- key_state_rows: bfloat16 [4096, 1024], P(('grp', 'uly')), may hold values from -6 to 6
- value_state_rows: bfloat16 [4096, 1024], P(('grp', 'uly')), may hold values from -6 to 6
- vert_blocks: int32 [64, 6], replicated, may hold values from -1 to 31, as said below
- slash_offsets: int32 [64, 3], replicated, may hold values from -1 to 4, as said below
Outputs:
- attended: bfloat16 [4096, 8192], P(('grp', 'uly'))
Inputs may be any that keep to these rules, and one draw needn't show every extreme that they name: `vert_blocks`: row h lists distinct block numbers first and -1 in the slots after them; every row lists one block or more and some row lists 6. `slash_offsets`: row h lists distinct offsets of at least 1 first and -1 in the slots after them; every row lists one offset or more and some row lists 3.
All inputs are finite; a program needn't handle non-finite values.
Results may differ from a plain program's by a relative error of at most 0.005.
Values may be sent and summed in bfloat16 or wider, within the bound.
A program may use at most 128 MiB of HBM per device.

v0:
```python
import functools

import jax
import jax.numpy as jnp
import numpy as np
from jax import lax
from jax.experimental import pallas as pl
from jax.experimental.pallas import tpu as pltpu
from jax.sharding import PartitionSpec as P

QUERY_HEADS = 64
KEY_VALUE_HEADS = 8
HEAD_SIZE = 128
BLOCK_TOKENS = 128


neg_large = -1e30


def passed_along(value, axis, steps):
    count = lax.axis_size(axis)
    initial, last = (max(0, -steps), min(count, count - steps))
    return lax.ppermute(value, axis, [(source, source + steps) for source in range(initial, last)])


def add_slot(running, slot_scores, allowed, weigh):
    best, total, accum = running
    slot_scores = jnp.where(allowed, slot_scores, neg_large)
    new_best = jnp.maximum(best, jnp.max(slot_scores, axis=-1))
    factor = jnp.exp(best - new_best)
    weights = jnp.where(allowed, jnp.exp(slot_scores - new_best[..., None]), 0.0)
    total = total * factor + jnp.sum(weights, axis=-1)
    accum = accum * factor[..., None] + weigh(weights.astype(jnp.bfloat16))
    return (new_best, total, accum)


def shards(queries, key_state_rows, value_state_rows, vert_blocks, slash_offsets):
    ulysses_count = lax.axis_size("uly")
    group_id = lax.axis_index("grp")
    uly_id = lax.axis_index("uly")
    per_device = QUERY_HEADS // ulysses_count
    group_width = QUERY_HEADS // KEY_VALUE_HEADS
    token_rows = queries.shape[0]
    ordering = jnp.arange(QUERY_HEADS, dtype=jnp.int32)
    heads_per_slot = np.arange(ulysses_count) * per_device // group_width
    key_outgoing = key_state_rows.reshape(token_rows, KEY_VALUE_HEADS, HEAD_SIZE)[
        :, heads_per_slot
    ].reshape(token_rows, ulysses_count * HEAD_SIZE)
    value_outgoing = value_state_rows.reshape(token_rows, KEY_VALUE_HEADS, HEAD_SIZE)[
        :, heads_per_slot
    ].reshape(token_rows, ulysses_count * HEAD_SIZE)
    q_group, k_group, v_group = (
        lax.all_to_all(queries, "uly", split_axis=1, concat_axis=0, tiled=True),
        lax.all_to_all(key_outgoing, "uly", split_axis=1, concat_axis=0, tiled=True),
        lax.all_to_all(value_outgoing, "uly", split_axis=1, concat_axis=0, tiled=True),
    )
    seg_rows = q_group.shape[0]
    block_count = seg_rows // BLOCK_TOKENS
    reach = block_count // 2
    q_tiles = q_group.reshape(block_count, BLOCK_TOKENS, per_device, HEAD_SIZE)
    key_block_tiles = k_group.reshape(block_count, BLOCK_TOKENS, HEAD_SIZE)
    value_block_tiles = v_group.reshape(block_count, BLOCK_TOKENS, HEAD_SIZE)
    prior_k, prior_v = passed_along(
        (key_block_tiles[block_count - reach :], value_block_tiles[block_count - reach :]), "grp", 1
    )
    k_wide = jnp.concatenate([prior_k, key_block_tiles], axis=0)
    v_wide = jnp.concatenate([prior_v, value_block_tiles], axis=0)
    heads_here = lax.dynamic_slice_in_dim(ordering, uly_id * per_device, per_device)
    vert_list = jnp.take(vert_blocks, heads_here, axis=0)
    offset_list = jnp.take(slash_offsets, heads_here, axis=0)
    local_block = jnp.where(vert_list >= 0, vert_list % block_count, 0)
    owned = (vert_list >= 0) & (vert_list // block_count == group_id)
    pick_k = jnp.where(
        owned[:, :, None, None], key_block_tiles[local_block], jnp.zeros((), jnp.bfloat16)
    )
    pick_v = jnp.where(
        owned[:, :, None, None], value_block_tiles[local_block], jnp.zeros((), jnp.bfloat16)
    )
    summed_k, summed_v = (
        lax.psum(pick_k.astype(jnp.float32).astype(jnp.bfloat16), "grp").astype(jnp.float32),
        lax.psum(pick_v.astype(jnp.float32).astype(jnp.bfloat16), "grp").astype(jnp.float32),
    )
    vert_k = summed_k.astype(jnp.bfloat16)
    vert_v = summed_v.astype(jnp.bfloat16)
    query_blocks = group_id * block_count + jnp.arange(block_count, dtype=jnp.int32)
    score_scale = HEAD_SIZE ** (-0.5)
    causal = (jnp.arange(BLOCK_TOKENS)[:, None] >= jnp.arange(BLOCK_TOKENS)[None, :])[
        None, :, None, :
    ]
    diag_scores = (
        jnp.einsum("nqhd,nkd->nqhk", q_tiles, key_block_tiles, preferred_element_type=jnp.float32)
        * score_scale
    )
    diag_scores = jnp.where(causal, diag_scores, neg_large)
    best = jnp.max(diag_scores, axis=-1)
    diag_weights = jnp.where(causal, jnp.exp(diag_scores - best[..., None]), 0.0)
    total = jnp.sum(diag_weights, axis=-1)
    accum = jnp.einsum(
        "nqhk,nkd->nqhd",
        diag_weights.astype(jnp.bfloat16),
        value_block_tiles,
        preferred_element_type=jnp.float32,
    )
    running = (best, total, accum)

    def slash_slot(slot_index, running):
        offset_now = lax.dynamic_index_in_dim(offset_list, slot_index, axis=1, keepdims=False)
        starts = jnp.where(offset_now >= 1, reach - offset_now, 0)

        def near_slice(begin_at):
            return (
                lax.dynamic_slice_in_dim(k_wide, begin_at, block_count, 0),
                lax.dynamic_slice_in_dim(v_wide, begin_at, block_count, 0),
            )

        k_near, v_near = jax.vmap(near_slice)(starts)
        allowed = (offset_now[None, :] >= 1) & (query_blocks[:, None] - offset_now[None, :] >= 0)
        slot_scores = (
            jnp.einsum("nqhd,hnkd->nqhk", q_tiles, k_near, preferred_element_type=jnp.float32)
            * score_scale
        )

        def weigh_near(prob_low):
            return jnp.einsum(
                "nqhk,hnkd->nqhd", prob_low, v_near, preferred_element_type=jnp.float32
            )

        return add_slot(running, slot_scores, allowed[:, None, :, None], weigh_near)

    slash_turns = jnp.max(jnp.sum((offset_list >= 1).astype(jnp.int32), axis=1))
    running = lax.fori_loop(0, slash_turns, slash_slot, running)

    def vert_slot(slot_index, running):
        block_now = lax.dynamic_index_in_dim(vert_list, slot_index, axis=1, keepdims=False)
        k_far = lax.dynamic_index_in_dim(vert_k, slot_index, axis=1, keepdims=False)
        v_far = lax.dynamic_index_in_dim(vert_v, slot_index, axis=1, keepdims=False)
        hits = (offset_list[None, :, :] >= 1) & (
            query_blocks[:, None, None] - offset_list[None, :, :] == block_now[None, :, None]
        )
        allowed = (
            (block_now[None, :] >= 0)
            & (block_now[None, :] < query_blocks[:, None])
            & jnp.logical_not(jnp.any(hits, axis=2))
        )
        slot_scores = (
            jnp.einsum("nqhd,hkd->nqhk", q_tiles, k_far, preferred_element_type=jnp.float32)
            * score_scale
        )

        def weigh_far(prob_low):
            return jnp.einsum("nqhk,hkd->nqhd", prob_low, v_far, preferred_element_type=jnp.float32)

        return add_slot(running, slot_scores, allowed[:, None, :, None], weigh_far)

    vert_turns = jnp.max(jnp.sum((vert_list >= 0).astype(jnp.int32), axis=1))
    best, total, accum = lax.fori_loop(0, vert_turns, vert_slot, running)
    mixed = (
        (accum / total[..., None]).astype(jnp.bfloat16).reshape(seg_rows, per_device * HEAD_SIZE)
    )
    returned = lax.all_to_all(mixed, "uly", split_axis=0, concat_axis=1, tiled=True)
    return returned


MESH = pl.DeviceIdType.MESH
GATHERED_BYTES_MAX = 1 << 25
LOG2_E = 1.4426950408889634
EARLY = ("zyx", "zxy")
LATE = ("yzx", "xzy")


def orders_of(head):
    return LATE if head % 3 == 1 else EARLY


def place_in(order, sizes, where):
    place = where["core"]
    for axis in reversed(order):
        place = place * sizes[axis] + where[axis]
    return place


def sizes_of(group_count, uly_count):
    return {"x": group_count // 2, "core": 2, "y": 2, "z": uly_count // 2}


def whereabouts(group, member):
    return {"x": group // 2, "core": group % 2, "y": member % 2, "z": member // 2}


def place_table(group_count, uly_count):
    block = np.arange(group_count * uly_count)
    where = whereabouts(block // uly_count, block % uly_count)
    sizes = sizes_of(group_count, uly_count)
    rows = [place_in(order, sizes, where) for order in EARLY + LATE]
    return np.stack(rows).astype(np.int32)


def attend_all(orders, q_ref, k_buf, v_buf, place_ref, vert_ref, slash_ref, out_ref, head, here):
    per_group = q_ref.shape[1] // (HEAD_SIZE * KEY_VALUE_HEADS)
    slash_slots, vert_slots = slash_ref.shape[0], vert_ref.shape[0]
    rate = HEAD_SIZE ** (-0.5) * LOG2_E
    causal = lax.broadcasted_iota(
        jnp.int32, (BLOCK_TOKENS, BLOCK_TOKENS), 0
    ) >= lax.broadcasted_iota(jnp.int32, (BLOCK_TOKENS, BLOCK_TOKENS), 1)
    k_row, v_row = ((EARLY + LATE).index(order) for order in orders)

    def slots_of(q_head):
        blocks, allowed = [here], [None]
        offsets = [slash_ref[slot, q_head] for slot in range(slash_slots)]
        for offset in offsets:
            ok = (offset >= 1) & (here - offset >= 0)
            blocks.append(jnp.where(ok, here - offset, here))
            allowed.append(ok)
        for slot in range(vert_slots):
            block = vert_ref[slot, q_head]
            ok = (block >= 0) & (block < here)
            for offset in offsets:
                ok = ok & jnp.logical_not((offset >= 1) & (here - offset == block))
            blocks.append(jnp.where(ok, block, here))
            allowed.append(ok)
        return blocks, allowed

    @pl.loop(0, per_group // GANG)
    def _(turn):
        chosen_slots, columns, scores = [], [], []
        for n in range(GANG):
            q_head = head * per_group + GANG * turn + n
            columns.append(pl.ds(pl.multiple_of(q_head * HEAD_SIZE, HEAD_SIZE), HEAD_SIZE))
            chosen_slots.append(slots_of(q_head))
        for n in range(GANG):
            blocks, _ = chosen_slots[n]
            keys = jnp.concatenate([k_buf[place_ref[k_row, block]] for block in blocks], axis=0)
            scores.append(
                lax.dot_general(
                    q_ref[:, columns[n]],
                    keys,
                    (((1,), (1,)), ((), ())),
                    preferred_element_type=jnp.float32,
                )
            )
        probs, totals = [], []
        for n in range(GANG):
            _, allowed = chosen_slots[n]
            pieces = []
            for slot, ok in enumerate(allowed):
                piece = scores[n][:, slot * BLOCK_TOKENS : (slot + 1) * BLOCK_TOKENS]
                if ok is None:
                    pieces.append(jnp.where(causal, piece, neg_large))
                else:
                    pieces.append(piece + jnp.where(ok, 0.0, neg_large).astype(jnp.float32))
            best = functools.reduce(jnp.maximum, pieces)
            best = jnp.max(best, axis=1, keepdims=True)
            weights = [jnp.exp2((piece - best) * rate) for piece in pieces]
            total = functools.reduce(jnp.add, weights)
            totals.append(jnp.sum(total, axis=1, keepdims=True))
            probs.append(
                jnp.concatenate([weight.astype(jnp.bfloat16) for weight in weights], axis=1)
            )
        for n in range(GANG):
            blocks, _ = chosen_slots[n]
            values = jnp.concatenate([v_buf[place_ref[v_row, block]] for block in blocks], axis=0)
            mixed = jnp.dot(probs[n], values, preferred_element_type=jnp.float32)
            out_ref[:, columns[n]] = (mixed / totals[n]).astype(out_ref.dtype)


GANG = 4
AHEAD = 1


def resident_kernel(
    group_count,
    uly_count,
    place_ref,
    vert_ref,
    slash_ref,
    q_hbm,
    k_ref,
    v_ref,
    out_hbm,
    q_ref,
    out_ref,
    q_sem,
    out_sem,
    own_sem,
    send_sem,
    recv_sem,
    *held,
):
    sizes = sizes_of(group_count, uly_count)
    group, member = lax.axis_index("grp"), lax.axis_index("uly")
    me = whereabouts(group, member)
    here = group * uly_count + member
    heads = KEY_VALUE_HEADS
    per_head = q_hbm.shape[1] // heads
    q_copy = pltpu.make_async_copy(q_hbm, q_ref, q_sem)
    q_copy.start()
    out_copies = []

    def device_at(where):
        return (where["x"] * 2 + where["core"], where["z"] * 2 + where["y"])

    peers, first, used = {}, {}, 0
    for axis in ("x", "y", "z", "core"):
        count = sizes[axis]
        peers[axis] = [
            device_at({**me, axis: lax.rem(me[axis] + d, count)}) for d in range(1, count)
        ]
        first[axis] = used
        used += count - 1

    barrier = pltpu.get_barrier_semaphore()
    everyone = [peer for group_peers in peers.values() for peer in group_peers]
    for peer in everyone:
        pl.semaphore_signal(barrier, inc=1, device_id=peer, device_id_type=MESH)
    pl.semaphore_wait(barrier, len(everyone))

    all_copies = []

    def sent(source, target, item, axis):
        copies = []
        for n, peer in enumerate(peers[axis]):
            copy = pltpu.make_async_remote_copy(
                src_ref=source,
                dst_ref=target,
                send_sem=send_sem.at[item, first[axis] + n],
                recv_sem=recv_sem.at[item, first[axis] + n],
                device_id=peer,
                device_id_type=MESH,
            )
            copy.start()
            copies.append(copy)
        all_copies.extend(copies)
        return copies

    flights, own = {}, {}

    def begin(head):
        for kind, source in enumerate((k_ref, v_ref)):
            item, order = 2 * head + kind, orders_of(head)[kind]
            slot = held[item].at[place_in(order, sizes, me)]
            columns = source.at[:, pl.ds(head * HEAD_SIZE, HEAD_SIZE)]
            flights[item] = sent(columns, slot, item, order[0])
            own[item] = pltpu.make_async_copy(columns, slot, own_sem.at[item])
            own[item].start()

    def forward(head, stage):
        for kind in range(2):
            item, order = 2 * head + kind, orders_of(head)[kind]
            if stage == 1:
                own[item].wait()
            for copy in flights[item]:
                copy.wait_recv()
            if stage <= 3:
                route = [*order, "core"]
                start = {**me, **{axis: 0 for axis in route[:stage]}}
                count = 1
                for axis in route[:stage]:
                    count *= sizes[axis]
                slab = held[item].at[pl.ds(place_in(order, sizes, start), count)]
                flights[item] = sent(slab, slab, item, route[stage])

    def along_z(head):
        if orders_of(head) == LATE:
            forward(head, 1)
        else:
            begin(head)

    for head in range(heads):
        if orders_of(head) == LATE:
            begin(head)
    for head in range(min(AHEAD, heads)):
        along_z(head)
    for step in range(heads + 3):
        if step + AHEAD < heads:
            along_z(step + AHEAD)
        if step < heads and orders_of(step) == EARLY:
            forward(step, 1)
        if 0 <= step - 1 < heads:
            forward(step - 1, 2)
        if 0 <= step - 3 < heads:
            head = step - 3
            forward(head, 4)
            if head == 0:
                q_copy.wait()
            attend_all(
                orders_of(head),
                q_ref,
                held[2 * head],
                held[2 * head + 1],
                place_ref,
                vert_ref,
                slash_ref,
                out_ref,
                head,
                here,
            )
            columns = pl.ds(head * per_head, per_head)
            out_copies.append(
                pltpu.make_async_copy(
                    out_ref.at[:, columns], out_hbm.at[:, columns], out_sem.at[head]
                )
            )
            out_copies[-1].start()
        if 0 <= step - 2 < heads:
            forward(step - 2, 3)
    for copy in all_copies:
        copy.wait_send()
    for copy in out_copies:
        copy.wait()


def resident_shards(queries, key_state_rows, value_state_rows, vert_blocks, slash_offsets):
    group_count, uly_count = lax.axis_size("grp"), lax.axis_size("uly")
    sizes = sizes_of(group_count, uly_count)
    copies = sum(count - 1 for count in sizes.values())
    items = 2 * KEY_VALUE_HEADS
    blocks = group_count * uly_count
    vmem = pl.BlockSpec(memory_space=pltpu.VMEM)
    smem = pl.BlockSpec(memory_space=pltpu.SMEM)
    hbm = pl.BlockSpec(memory_space=pl.ANY)
    return pl.pallas_call(
        functools.partial(resident_kernel, group_count, uly_count),
        out_shape=jax.ShapeDtypeStruct(queries.shape, queries.dtype),
        in_specs=[smem, smem, smem, hbm, vmem, vmem],
        out_specs=hbm,
        scratch_shapes=[
            pltpu.VMEM(queries.shape, queries.dtype),
            pltpu.VMEM(queries.shape, queries.dtype),
            pltpu.SemaphoreType.DMA,
            pltpu.SemaphoreType.DMA((KEY_VALUE_HEADS,)),
            pltpu.SemaphoreType.DMA((items,)),
            pltpu.SemaphoreType.DMA((items, copies)),
            pltpu.SemaphoreType.DMA((items, copies)),
        ]
        + [pltpu.VMEM((blocks, BLOCK_TOKENS, HEAD_SIZE), key_state_rows.dtype)] * items,
        compiler_params=pltpu.CompilerParams(collective_id=0, has_side_effects=True),
        name="gather_and_attend",
    )(
        jnp.asarray(place_table(group_count, uly_count)),
        vert_blocks.T,
        slash_offsets.T,
        queries,
        key_state_rows,
        value_state_rows,
    )


def chosen(queries, key_state_rows, *rest):
    devices = lax.axis_size("grp") * lax.axis_size("uly")
    gathered_bytes = 2 * devices * key_state_rows.size * key_state_rows.dtype.itemsize
    fits = gathered_bytes <= GATHERED_BYTES_MAX and queries.shape[0] == BLOCK_TOKENS
    plan = resident_shards if fits else shards
    return plan(queries, key_state_rows, *rest)


def solution(mesh):
    return jax.shard_map(
        chosen,
        mesh=mesh,
        in_specs=(
            P(("grp", "uly"), None),
            P(("grp", "uly"), None),
            P(("grp", "uly"), None),
            P(),
            P(),
        ),
        out_specs=P(("grp", "uly"), None),
        check_vma=False,
    )
```

profile of v0, /device:TPU:0, one launch (start us, length us, event | category | flops | bytes accessed | tf_op | source)
XLA Modules:
  0.0 96.1 jit_solution(15843957523084097958)
XLA Ops:
  0.0 93.0 %gather_and_attend.1 = bf16[128,8192]{1,0:T(8,128)(2,1)} custom-call(s32[4,32]{1,0:T(4,128)} %constant.2.clone.place_ref, s32[6,64]{1,0:T(8,128)} %bitcast.2, s32[3,64]{1,0:T(4,128)} %bitcast.3, bf16[128,8192]{1,0:T(8,128)(2,1)} %q_hbm.1, bf16[128,1024]{1,0:T(8,128)(2,1)} %k_ref.1, bf16[128,1024]{1,0:T(8,128)(2,1)} %v_ref.1), custom_call_target="tpu_custom_call" | custom-call | tf_op jit(solution)/shard_map/gather_and_attend/pallas_call | solution.py:421
  93.0 3.1 %copy.8 = bf16[128,8192]{1,0:T(8,128)(2,1)} copy(bf16[128,8192]{1,0:T(8,128)(2,1)} %gather_and_attend.1) | data formatting | bytes 4194304
where the time goes:
time: 96.2 us; the launch traced here: 96.1 us
  Pallas kernels  93 us (97%)
  local copies, waits for them, and re-layouts  3.1 us (3%)
    pallas_call x1, Pallas kernels, resident_shards(): pl.pallas_call(functools.partial(resident_kernel, group_count, uly_count)...  93 us
    unnamed x1, local copies, waits for them, and re-layouts  3.1 us

commit v1 on v0

v1 whole, which is shorter than its diff:
```python
import functools

import jax
import jax.numpy as jnp
import numpy as np
from jax import lax
from jax.experimental import pallas as pl
from jax.experimental.pallas import tpu as pltpu
from jax.sharding import PartitionSpec as P

QUERY_HEADS = 64
KEY_VALUE_HEADS = 8
HEAD_SIZE = 128
BLOCK_TOKENS = 128


neg_large = -1e30


def passed_along(value, axis, steps):
    count = lax.axis_size(axis)
    initial, last = (max(0, -steps), min(count, count - steps))
    return lax.ppermute(value, axis, [(source, source + steps) for source in range(initial, last)])


def add_slot(running, slot_scores, allowed, weigh):
    best, total, accum = running
    slot_scores = jnp.where(allowed, slot_scores, neg_large)
    new_best = jnp.maximum(best, jnp.max(slot_scores, axis=-1))
    factor = jnp.exp(best - new_best)
    weights = jnp.where(allowed, jnp.exp(slot_scores - new_best[..., None]), 0.0)
    total = total * factor + jnp.sum(weights, axis=-1)
    accum = accum * factor[..., None] + weigh(weights.astype(jnp.bfloat16))
    return (new_best, total, accum)


def shards(queries, key_state_rows, value_state_rows, vert_blocks, slash_offsets):
    ulysses_count = lax.axis_size("uly")
    group_id = lax.axis_index("grp")
    uly_id = lax.axis_index("uly")
    per_device = QUERY_HEADS // ulysses_count
    group_width = QUERY_HEADS // KEY_VALUE_HEADS
    token_rows = queries.shape[0]
    ordering = jnp.arange(QUERY_HEADS, dtype=jnp.int32)
    heads_per_slot = np.arange(ulysses_count) * per_device // group_width
    key_outgoing = key_state_rows.reshape(token_rows, KEY_VALUE_HEADS, HEAD_SIZE)[
        :, heads_per_slot
    ].reshape(token_rows, ulysses_count * HEAD_SIZE)
    value_outgoing = value_state_rows.reshape(token_rows, KEY_VALUE_HEADS, HEAD_SIZE)[
        :, heads_per_slot
    ].reshape(token_rows, ulysses_count * HEAD_SIZE)
    q_group, k_group, v_group = (
        lax.all_to_all(queries, "uly", split_axis=1, concat_axis=0, tiled=True),
        lax.all_to_all(key_outgoing, "uly", split_axis=1, concat_axis=0, tiled=True),
        lax.all_to_all(value_outgoing, "uly", split_axis=1, concat_axis=0, tiled=True),
    )
    seg_rows = q_group.shape[0]
    block_count = seg_rows // BLOCK_TOKENS
    reach = block_count // 2
    q_tiles = q_group.reshape(block_count, BLOCK_TOKENS, per_device, HEAD_SIZE)
    key_block_tiles = k_group.reshape(block_count, BLOCK_TOKENS, HEAD_SIZE)
    value_block_tiles = v_group.reshape(block_count, BLOCK_TOKENS, HEAD_SIZE)
    prior_k, prior_v = passed_along(
        (key_block_tiles[block_count - reach :], value_block_tiles[block_count - reach :]), "grp", 1
    )
    k_wide = jnp.concatenate([prior_k, key_block_tiles], axis=0)
    v_wide = jnp.concatenate([prior_v, value_block_tiles], axis=0)
    heads_here = lax.dynamic_slice_in_dim(ordering, uly_id * per_device, per_device)
    vert_list = jnp.take(vert_blocks, heads_here, axis=0)
    offset_list = jnp.take(slash_offsets, heads_here, axis=0)
    local_block = jnp.where(vert_list >= 0, vert_list % block_count, 0)
    owned = (vert_list >= 0) & (vert_list // block_count == group_id)
    pick_k = jnp.where(
        owned[:, :, None, None], key_block_tiles[local_block], jnp.zeros((), jnp.bfloat16)
    )
    pick_v = jnp.where(
        owned[:, :, None, None], value_block_tiles[local_block], jnp.zeros((), jnp.bfloat16)
    )
    summed_k, summed_v = (
        lax.psum(pick_k.astype(jnp.float32).astype(jnp.bfloat16), "grp").astype(jnp.float32),
        lax.psum(pick_v.astype(jnp.float32).astype(jnp.bfloat16), "grp").astype(jnp.float32),
    )
    vert_k = summed_k.astype(jnp.bfloat16)
    vert_v = summed_v.astype(jnp.bfloat16)
    query_blocks = group_id * block_count + jnp.arange(block_count, dtype=jnp.int32)
    score_scale = HEAD_SIZE ** (-0.5)
    causal = (jnp.arange(BLOCK_TOKENS)[:, None] >= jnp.arange(BLOCK_TOKENS)[None, :])[
        None, :, None, :
    ]
    diag_scores = (
        jnp.einsum("nqhd,nkd->nqhk", q_tiles, key_block_tiles, preferred_element_type=jnp.float32)
        * score_scale
    )
    diag_scores = jnp.where(causal, diag_scores, neg_large)
    best = jnp.max(diag_scores, axis=-1)
    diag_weights = jnp.where(causal, jnp.exp(diag_scores - best[..., None]), 0.0)
    total = jnp.sum(diag_weights, axis=-1)
    accum = jnp.einsum(
        "nqhk,nkd->nqhd",
        diag_weights.astype(jnp.bfloat16),
        value_block_tiles,
        preferred_element_type=jnp.float32,
    )
    running = (best, total, accum)

    def slash_slot(slot_index, running):
        offset_now = lax.dynamic_index_in_dim(offset_list, slot_index, axis=1, keepdims=False)
        starts = jnp.where(offset_now >= 1, reach - offset_now, 0)

        def near_slice(begin_at):
            return (
                lax.dynamic_slice_in_dim(k_wide, begin_at, block_count, 0),
                lax.dynamic_slice_in_dim(v_wide, begin_at, block_count, 0),
            )

        k_near, v_near = jax.vmap(near_slice)(starts)
        allowed = (offset_now[None, :] >= 1) & (query_blocks[:, None] - offset_now[None, :] >= 0)
        slot_scores = (
            jnp.einsum("nqhd,hnkd->nqhk", q_tiles, k_near, preferred_element_type=jnp.float32)
            * score_scale
        )

        def weigh_near(prob_low):
            return jnp.einsum(
                "nqhk,hnkd->nqhd", prob_low, v_near, preferred_element_type=jnp.float32
            )

        return add_slot(running, slot_scores, allowed[:, None, :, None], weigh_near)

    slash_turns = jnp.max(jnp.sum((offset_list >= 1).astype(jnp.int32), axis=1))
    running = lax.fori_loop(0, slash_turns, slash_slot, running)

    def vert_slot(slot_index, running):
        block_now = lax.dynamic_index_in_dim(vert_list, slot_index, axis=1, keepdims=False)
        k_far = lax.dynamic_index_in_dim(vert_k, slot_index, axis=1, keepdims=False)
        v_far = lax.dynamic_index_in_dim(vert_v, slot_index, axis=1, keepdims=False)
        hits = (offset_list[None, :, :] >= 1) & (
            query_blocks[:, None, None] - offset_list[None, :, :] == block_now[None, :, None]
        )
        allowed = (
            (block_now[None, :] >= 0)
            & (block_now[None, :] < query_blocks[:, None])
            & jnp.logical_not(jnp.any(hits, axis=2))
        )
        slot_scores = (
            jnp.einsum("nqhd,hkd->nqhk", q_tiles, k_far, preferred_element_type=jnp.float32)
            * score_scale
        )

        def weigh_far(prob_low):
            return jnp.einsum("nqhk,hkd->nqhd", prob_low, v_far, preferred_element_type=jnp.float32)

        return add_slot(running, slot_scores, allowed[:, None, :, None], weigh_far)

    vert_turns = jnp.max(jnp.sum((vert_list >= 0).astype(jnp.int32), axis=1))
    best, total, accum = lax.fori_loop(0, vert_turns, vert_slot, running)
    mixed = (
        (accum / total[..., None]).astype(jnp.bfloat16).reshape(seg_rows, per_device * HEAD_SIZE)
    )
    returned = lax.all_to_all(mixed, "uly", split_axis=0, concat_axis=1, tiled=True)
    return returned


MESH = pl.DeviceIdType.MESH
LOG2_E = 1.4426950408889634
HALVES = 2
FOUR = 4
NEAR = ((0, 1), (1, 0), (1, 1))


def axis_pair(half):
    return ("y", "x") if half == 0 else ("x", "y")


def whereabouts(group, member):
    return {"x": group // 2, "core": group % 2, "y": member % 2, "z": member // 2}


def host_of(half, where):
    shared, _ = axis_pair(half)
    return where[shared] * 2 + where["core"]


def place_of(half, where, length):
    shared, other = axis_pair(half)
    major, minor = ("core", shared) if half == 0 else (shared, "core")
    return ((where[major] * length + where["z"]) * 2 + where[other]) * 2 + where[minor]


def place_table(group_count, uly_count):
    block = np.arange(group_count * uly_count)
    where = whereabouts(block // uly_count, block % uly_count)
    rows = [place_of(half, where, uly_count // 2) for half in range(HALVES)]
    return np.stack(rows).astype(np.int32)


def flipped(where, axis, by):
    return {**where, axis: 1 - where[axis]} if by else where


def attend(row, q_refs, k_buf, v_buf, place_ref, vert_ref, slash_ref, o_refs, q_head, turn, places):
    slash_slots, vert_slots = slash_ref.shape[0], vert_ref.shape[0]
    rate = HEAD_SIZE ** (-0.5) * LOG2_E
    causal = lax.broadcasted_iota(
        jnp.int32, (BLOCK_TOKENS, BLOCK_TOKENS), 0
    ) >= lax.broadcasted_iota(jnp.int32, (BLOCK_TOKENS, BLOCK_TOKENS), 1)
    columns = pl.ds(turn * HEAD_SIZE, HEAD_SIZE)
    offsets = [slash_ref[slot, q_head] for slot in range(slash_slots)]
    listed = [vert_ref[slot, q_head] for slot in range(vert_slots)]

    def slots_of(here):
        blocks, allowed = [here], [None]
        for offset in offsets:
            ok = (offset >= 1) & (here - offset >= 0)
            blocks.append(jnp.where(ok, here - offset, here))
            allowed.append(ok)
        for block in listed:
            ok = (block >= 0) & (block < here)
            for offset in offsets:
                ok = ok & jnp.logical_not((offset >= 1) & (here - offset == block))
            blocks.append(jnp.where(ok, block, here))
            allowed.append(ok)
        return blocks, allowed

    chosen_slots = [slots_of(here) for here in places]
    scores, probs, totals = [], [], []
    for q_ref, (blocks, _) in zip(q_refs, chosen_slots):
        keys = jnp.concatenate([k_buf[place_ref[row, block]] for block in blocks], axis=0)
        scores.append(
            lax.dot_general(
                q_ref[:, columns],
                keys,
                (((1,), (1,)), ((), ())),
                preferred_element_type=jnp.float32,
            )
        )
    for score, (_, allowed) in zip(scores, chosen_slots):
        pieces = []
        for slot, ok in enumerate(allowed):
            piece = score[:, slot * BLOCK_TOKENS : (slot + 1) * BLOCK_TOKENS]
            if ok is None:
                pieces.append(jnp.where(causal, piece, neg_large))
            else:
                pieces.append(piece + jnp.where(ok, 0.0, neg_large).astype(jnp.float32))
        best = functools.reduce(jnp.maximum, pieces)
        best = jnp.max(best, axis=1, keepdims=True)
        weights = [jnp.exp2((piece - best) * rate) for piece in pieces]
        total = functools.reduce(jnp.add, weights)
        totals.append(jnp.sum(total, axis=1, keepdims=True))
        probs.append(jnp.concatenate([weight.astype(jnp.bfloat16) for weight in weights], axis=1))
    for o_ref, prob, total, (blocks, _) in zip(o_refs, probs, totals, chosen_slots):
        values = jnp.concatenate([v_buf[place_ref[row, block]] for block in blocks], axis=0)
        mixed = jnp.dot(prob, values, preferred_element_type=jnp.float32)
        o_ref[:, columns] = (mixed / total).astype(o_ref.dtype)


def split_kernel(
    uly_count,
    place_ref,
    vert_ref,
    slash_ref,
    q_hbm,
    k_hbm,
    v_hbm,
    out_hbm,
    k_own,
    v_own,
    load_sem,
    own_sem,
    ex_send,
    ex_recv,
    q_sem,
    q_send,
    q_recv,
    g_send,
    g_recv,
    o_sem,
    o_send,
    o_recv,
    *buffers,
):
    length = uly_count // 2
    group, member = lax.axis_index("grp"), lax.axis_index("uly")
    me = whereabouts(group, member)
    z = me["z"]
    per_kv = q_hbm.shape[1] // KEY_VALUE_HEADS
    turns = per_kv // HEAD_SIZE
    held = buffers[:4]
    q_bufs = (buffers[4:8], buffers[8:12])
    o_bufs = (buffers[12:16], buffers[16:20])
    sources = (k_own, v_own)

    def block_at(where):
        return (where["x"] * 2 + where["core"]) * uly_count + where["z"] * 2 + where["y"]

    def device_at(where):
        return (where["x"] * 2 + where["core"], where["z"] * 2 + where["y"])

    def relative(half, steps):
        shared, _ = axis_pair(half)
        return flipped(flipped(me, shared, steps[0]), "core", steps[1])

    def kv_head(half, where):
        return half * FOUR + host_of(half, where)

    def lanes(start, width):
        return pl.ds(pl.multiple_of(start, HEAD_SIZE), width)

    loads = []
    for n, (source, target) in enumerate(((k_hbm, k_own), (v_hbm, v_own))):
        loads.append(pltpu.make_async_copy(source, target, load_sem.at[n]))
        loads[-1].start()
    own = []
    for half in range(HALVES):
        for kind, source in enumerate((k_hbm, v_hbm)):
            item = 2 * half + kind
            columns = lanes(kv_head(half, me) * HEAD_SIZE, HEAD_SIZE)
            own.append(
                pltpu.make_async_copy(
                    source.at[:, columns],
                    held[item].at[place_of(half, me, length)],
                    own_sem.at[item],
                )
            )
            own[-1].start()
    q_own = []
    for half in range(HALVES):
        columns = lanes(kv_head(half, me) * per_kv, per_kv)
        q_own.append(
            pltpu.make_async_copy(q_hbm.at[:, columns], q_bufs[half][0], q_sem.at[half])
        )
        q_own[-1].start()

    barrier = pltpu.get_barrier_semaphore()
    around = [relative(half, steps) for half in range(HALVES) for steps in NEAR]
    around = around[:3] + around[4:]
    for where in around:
        pl.semaphore_signal(barrier, inc=1, device_id=device_at(where), device_id_type=MESH)

    def greet(step):
        pl.semaphore_signal(
            barrier, inc=1, device_id=device_at({**me, "z": z + step}), device_id_type=MESH
        )

    pl.when(z > 0)(lambda: greet(-1))
    pl.when(z < length - 1)(lambda: greet(1))
    count = len(around) + jnp.where(z > 0, 1, 0) + jnp.where(z < length - 1, 1, 0)
    pl.semaphore_wait(barrier, count)
    for load in loads:
        load.wait()

    def remote(source, target, send, recv, where):
        return pltpu.make_async_remote_copy(
            src_ref=source,
            dst_ref=target,
            send_sem=send,
            recv_sem=recv,
            device_id=device_at(where),
            device_id_type=MESH,
        )

    sent = []

    def begin(copy):
        copy.start()
        sent.append(copy)
        return copy

    exchanged = {}

    def exchange(half):
        for kind in range(2):
            item = 2 * half + kind
            for n, steps in enumerate(NEAR):
                peer = relative(half, steps)
                columns = lanes(kv_head(half, peer) * HEAD_SIZE, HEAD_SIZE)
                exchanged[item, n] = begin(
                    remote(
                        sources[kind].at[:, columns],
                        held[item].at[place_of(half, me, length)],
                        ex_send.at[item, n],
                        ex_recv.at[item, n],
                        peer,
                    )
                )

    asked = {}

    def ask(half):
        for n, steps in enumerate(NEAR):
            peer = relative(half, steps)
            columns = lanes(kv_head(half, peer) * per_kv, per_kv)
            asked[half, n] = begin(
                remote(
                    q_hbm.at[:, columns],
                    q_bufs[half][n + 1],
                    q_send.at[half, n],
                    q_recv.at[half, n],
                    peer,
                )
            )

    def hop(item, major, slab, way):
        half = item // 2
        _, other = axis_pair(half)
        first = ((major * length + slab) * 2 + me[other]) * 2
        part = held[item].at[pl.ds(first, 2)]
        if way == 2:
            where, lane = {**me, other: 1 - me[other]}, 1
        else:
            where, lane = {**me, "z": z + (1 if way == 0 else -1)}, 0
        return remote(
            part, part, g_send.at[item, major, slab, way], g_recv.at[item, major, slab, lane], where
        )

    def arrived(item, major, slab, lane):
        half = item // 2
        _, other = axis_pair(half)
        side = me[other] if lane == 0 else 1 - me[other]
        first = ((major * length + slab) * 2 + side) * 2
        part = held[item].at[pl.ds(first, 2)]
        remote(
            part, part, g_send.at[item, major, slab, 0], g_recv.at[item, major, slab, lane], me
        ).wait_recv()

    def ways(item, kind):
        up = (0, z < length - 1)
        down = (1, z > 0)
        across = (2, None if item >= 2 else me["x"] == 0)
        return {"own": (up, down, across), "below": (up, across), "above": (down, across)}[kind]

    def each_way(item, major, slab, kind, act):
        for way, ok in ways(item, kind):
            if ok is None:
                act(hop(item, major, slab, way))
            else:
                pl.when(ok)(lambda way=way: act(hop(item, major, slab, way)))

    def start(item, major, slab, kind):
        each_way(item, major, slab, kind, lambda copy: copy.start())

    def launch(item):
        own[item].wait()
        for n in range(len(NEAR)):
            exchanged[item, n].wait_recv()
        for major in range(2):
            start(item, major, z, "own")

    def step(item, major, distance):
        @pl.when(z >= distance)
        def _():
            arrived(item, major, z - distance, 0)
            start(item, major, z - distance, "below")

        @pl.when(z + distance < length)
        def _():
            arrived(item, major, z + distance, 0)
            start(item, major, z + distance, "above")

    def settle(item):
        def crossing():
            for major in range(2):
                for slab in range(length):
                    arrived(item, major, slab, 1)

        if item >= 2:
            crossing()
        else:
            pl.when(me["x"] == 1)(crossing)

    def drain(item):
        for major in range(2):
            each_way(item, major, z, "own", lambda copy: copy.wait_send())
            for distance in range(1, length):
                @pl.when(z >= distance)
                def _():
                    each_way(
                        item, major, z - distance, "below", lambda copy: copy.wait_send()
                    )

                @pl.when(z + distance < length)
                def _():
                    each_way(
                        item, major, z + distance, "above", lambda copy: copy.wait_send()
                    )

    answered = []

    def answer(half, turn):
        columns = lanes(kv_head(half, me) * per_kv + turn * HEAD_SIZE, HEAD_SIZE)
        local = pl.ds(turn * HEAD_SIZE, HEAD_SIZE)
        for n, steps in enumerate(NEAR):
            copy = begin(
                remote(
                    o_bufs[half][n + 1].at[:, local],
                    out_hbm.at[:, columns],
                    o_send.at[half, turn, n],
                    o_recv.at[half, turn, n],
                    relative(half, steps),
                )
            )
            answered.append(copy)
        copy = pltpu.make_async_copy(
            o_bufs[half][0].at[:, local], out_hbm.at[:, columns], o_sem.at[half, turn]
        )
        copy.start()
        own_out.append(copy)

    own_out = []
    where_from = ((0, 0),) + NEAR

    def compute(half, turn):
        places = [block_at(relative(half, steps)) for steps in where_from]
        attend(
            half,
            q_bufs[half],
            held[2 * half],
            held[2 * half + 1],
            place_ref,
            vert_ref,
            slash_ref,
            o_bufs[half],
            kv_head(half, me) * turns + turn,
            turn,
            places,
        )
        answer(half, turn)

    def steps_of(half, distance):
        return [(2 * half + kind, major, distance) for kind in range(2) for major in range(2)]

    exchange(0)
    exchange(1)
    ask(0)
    launch(0)
    launch(1)
    for distance in range(1, length - 1):
        for args in steps_of(0, distance):
            step(*args)
    launch(2)
    launch(3)
    for args in steps_of(0, length - 1):
        step(*args)
    ask(1)
    pending = [args for distance in range(1, length) for args in steps_of(1, distance)]
    for args in pending[:2]:
        step(*args)
    pending = pending[2:]
    settle(0)
    settle(1)
    q_own[0].wait()
    for n in range(len(NEAR)):
        asked[0, n].wait_recv()
    for turn in range(turns):
        compute(0, turn)
        for args in pending[:1]:
            step(*args)
        pending = pending[1:]
    for args in pending:
        step(*args)
    settle(2)
    settle(3)
    q_own[1].wait()
    for n in range(len(NEAR)):
        asked[1, n].wait_recv()
    for turn in range(turns):
        compute(1, turn)
    for copy in sent:
        copy.wait_send()
    for item in range(4):
        drain(item)
    for copy in answered:
        copy.wait_recv()
    for copy in own_out:
        copy.wait()


def split_shards(queries, key_state_rows, value_state_rows, vert_blocks, slash_offsets):
    group_count, uly_count = lax.axis_size("grp"), lax.axis_size("uly")
    blocks = group_count * uly_count
    length = uly_count // 2
    turns = QUERY_HEADS // KEY_VALUE_HEADS
    near = len(NEAR)
    dtype = queries.dtype
    smem = pl.BlockSpec(memory_space=pltpu.SMEM)
    hbm = pl.BlockSpec(memory_space=pl.ANY)
    dma = pltpu.SemaphoreType.DMA
    share = (BLOCK_TOKENS, turns * HEAD_SIZE)
    return pl.pallas_call(
        functools.partial(split_kernel, uly_count),
        out_shape=jax.ShapeDtypeStruct(queries.shape, dtype),
        in_specs=[smem, smem, smem, hbm, hbm, hbm],
        out_specs=hbm,
        scratch_shapes=[
            pltpu.VMEM(key_state_rows.shape, dtype),
            pltpu.VMEM(value_state_rows.shape, dtype),
            dma((2,)),
            dma((4,)),
            dma((4, near)),
            dma((4, near)),
            dma((HALVES,)),
            dma((HALVES, near)),
            dma((HALVES, near)),
            dma((4, 2, length, 3)),
            dma((4, 2, length, 2)),
            dma((HALVES, turns)),
            dma((HALVES, turns, near)),
            dma((HALVES, turns, near)),
        ]
        + [pltpu.VMEM((blocks, BLOCK_TOKENS, HEAD_SIZE), dtype)] * 4
        + [pltpu.VMEM(share, dtype)] * (4 * HALVES * 2),
        compiler_params=pltpu.CompilerParams(collective_id=0, has_side_effects=True),
        name="split_and_attend",
    )(
        jnp.asarray(place_table(group_count, uly_count)),
        vert_blocks.T,
        slash_offsets.T,
        queries,
        key_state_rows,
        value_state_rows,
    )


def chosen(queries, key_state_rows, *rest):
    group_count, uly_count = lax.axis_size("grp"), lax.axis_size("uly")
    fits = (
        group_count == FOUR
        and uly_count == 2 * FOUR
        and KEY_VALUE_HEADS == HALVES * FOUR
        and queries.shape[0] == BLOCK_TOKENS
    )
    plan = split_shards if fits else shards
    return plan(queries, key_state_rows, *rest)


def solution(mesh):
    return jax.shard_map(
        chosen,
        mesh=mesh,
        in_specs=(
            P(("grp", "uly"), None),
            P(("grp", "uly"), None),
            P(("grp", "uly"), None),
            P(),
            P(),
        ),
        out_specs=P(("grp", "uly"), None),
        check_vma=False,
    )
```

time: 96.2 us -> 81 us (0.84)
  Pallas kernels: 93 us -> 77.7 us
    pallas_call x1, Pallas kernels: 93 us -> 77.7 us  [split_shards(): pl.pallas_call(functools.partial(split_kernel, uly_count), out_shape=jax....]
where the time goes in v1:
time: 81 us; the launch traced here: 80.8 us
  Pallas kernels  77.7 us (96%)
  local copies, waits for them, and re-layouts  3.1 us (4%)
    pallas_call x1, Pallas kernels, split_shards(): pl.pallas_call(functools.partial(split_kernel, uly_count), out_shape=jax....  77.7 us
    unnamed x1, local copies, waits for them, and re-layouts  3.1 us

profile of v1, /device:TPU:0, one launch (start us, length us, event | category | flops | bytes accessed | tf_op | source)
XLA Modules:
  0.0 80.8 jit_solution(11735205274929083333)
XLA Ops:
  0.0 77.7 %split_and_attend.1 = bf16[128,8192]{1,0:T(8,128)(2,1)} custom-call(s32[2,32]{1,0:T(2,128)} %constant.2.clone.place_ref, s32[6,64]{1,0:T(8,128)} %bitcast.2, s32[3,64]{1,0:T(4,128)} %bitcast.3, bf16[128,8192]{1,0:T(8,128)(2,1)} %q_hbm.1, bf16[128,1024]{1,0:T(8,128)(2,1)} %k_hbm.1, bf16[128,1024]{1,0:T(8,128)(2,1)} %v_hbm.1), custom_call_target="tpu_custom_call" | custom-call | tf_op jit(solution)/shard_map/split_and_attend/pallas_call | solution.py:589
  77.7 3.1 %copy.8 = bf16[128,8192]{1,0:T(8,128)(2,1)} copy(bf16[128,8192]{1,0:T(8,128)(2,1)} %split_and_attend.1) | data formatting | bytes 4194304

commit v2 on v1

--- a/solution.py
+++ b/solution.py
@@ -164,8 +164,9 @@
 MESH = pl.DeviceIdType.MESH
 LOG2_E = 1.4426950408889634
 HALVES = 2
-FOUR = 4
-NEAR = ((0, 1), (1, 0), (1, 1))
+PHASES = ((0, 0), (1, 0), (0, 1), (1, 1))
+UP, DOWN, ACROSS, BESIDE, BESIDE_TOO = range(5)
+GANG = 2
 
 
 def axis_pair(half):
@@ -176,15 +177,13 @@
     return {"x": group // 2, "core": group % 2, "y": member % 2, "z": member // 2}
 
 
-def host_of(half, where):
-    shared, _ = axis_pair(half)
-    return where[shared] * 2 + where["core"]
+def flipped(where, axis):
+    return {**where, axis: 1 - where[axis]}
 
 
 def place_of(half, where, length):
     shared, other = axis_pair(half)
-    major, minor = ("core", shared) if half == 0 else (shared, "core")
-    return ((where[major] * length + where["z"]) * 2 + where[other]) * 2 + where[minor]
+    return ((where["core"] * length + where["z"]) * 2 + where[other]) * 2 + where[shared]
 
 
 def place_table(group_count, uly_count):
@@ -194,27 +193,22 @@
     return np.stack(rows).astype(np.int32)
 
 
-def flipped(where, axis, by):
-    return {**where, axis: 1 - where[axis]} if by else where
-
-
-def attend(row, q_refs, k_buf, v_buf, place_ref, vert_ref, slash_ref, o_refs, q_head, turn, places):
+def attend(row, units, k_buf, v_buf, place_ref, vert_ref, slash_ref):
     slash_slots, vert_slots = slash_ref.shape[0], vert_ref.shape[0]
     rate = HEAD_SIZE ** (-0.5) * LOG2_E
     causal = lax.broadcasted_iota(
         jnp.int32, (BLOCK_TOKENS, BLOCK_TOKENS), 0
     ) >= lax.broadcasted_iota(jnp.int32, (BLOCK_TOKENS, BLOCK_TOKENS), 1)
-    columns = pl.ds(turn * HEAD_SIZE, HEAD_SIZE)
-    offsets = [slash_ref[slot, q_head] for slot in range(slash_slots)]
-    listed = [vert_ref[slot, q_head] for slot in range(vert_slots)]
-
-    def slots_of(here):
+
+    def slots_of(q_head, here):
         blocks, allowed = [here], [None]
+        offsets = [slash_ref[slot, q_head] for slot in range(slash_slots)]
         for offset in offsets:
             ok = (offset >= 1) & (here - offset >= 0)
             blocks.append(jnp.where(ok, here - offset, here))
             allowed.append(ok)
-        for block in listed:
+        for slot in range(vert_slots):
+            block = vert_ref[slot, q_head]
             ok = (block >= 0) & (block < here)
             for offset in offsets:
                 ok = ok & jnp.logical_not((offset >= 1) & (here - offset == block))
@@ -222,9 +216,9 @@
             allowed.append(ok)
         return blocks, allowed
 
-    chosen_slots = [slots_of(here) for here in places]
+    chosen_slots = [slots_of(q_head, here) for _, _, _, q_head, here in units]
     scores, probs, totals = [], [], []
-    for q_ref, (blocks, _) in zip(q_refs, chosen_slots):
+    for (q_ref, _, columns, _, _), (blocks, _) in zip(units, chosen_slots):
         keys = jnp.concatenate([k_buf[place_ref[row, block]] for block in blocks], axis=0)
         scores.append(
             lax.dot_general(
@@ -248,7 +242,9 @@
         total = functools.reduce(jnp.add, weights)
         totals.append(jnp.sum(total, axis=1, keepdims=True))
         probs.append(jnp.concatenate([weight.astype(jnp.bfloat16) for weight in weights], axis=1))
-    for o_ref, prob, total, (blocks, _) in zip(o_refs, probs, totals, chosen_slots):
+    for (_, o_ref, columns, _, _), prob, total, (blocks, _) in zip(
+        units, probs, totals, chosen_slots
+    ):
         values = jnp.concatenate([v_buf[place_ref[row, block]] for block in blocks], axis=0)
         mixed = jnp.dot(prob, values, preferred_element_type=jnp.float32)
         o_ref[:, columns] = (mixed / total).astype(o_ref.dtype)
@@ -274,6 +270,7 @@
     q_recv,
     g_send,
     g_recv,
+    b_recv,
     o_sem,
     o_send,
     o_recv,
@@ -285,9 +282,10 @@
     z = me["z"]
     per_kv = q_hbm.shape[1] // KEY_VALUE_HEADS
     turns = per_kv // HEAD_SIZE
-    held = buffers[:4]
-    q_bufs = (buffers[4:8], buffers[8:12])
-    o_bufs = (buffers[12:16], buffers[16:20])
+    gangs = turns // GANG
+    held = buffers[:8]
+    q_bufs = [buffers[8 + 2 * n : 10 + 2 * n] for n in range(4)]
+    o_bufs = [buffers[16 + 2 * n : 18 + 2 * n] for n in range(4)]
     sources = (k_own, v_own)
 
     def block_at(where):
@@ -296,12 +294,11 @@
     def device_at(where):
         return (where["x"] * 2 + where["core"], where["z"] * 2 + where["y"])
 
-    def relative(half, steps):
-        shared, _ = axis_pair(half)
-        return flipped(flipped(me, shared, steps[0]), "core", steps[1])
-
-    def kv_head(half, where):
-        return half * FOUR + host_of(half, where)
+    def partner(half):
+        return flipped(me, axis_pair(half)[0])
+
+    def kv_head(half, n, where):
+        return (half * 2 + where[axis_pair(half)[0]]) * 2 + n
 
     def lanes(start, width):
         return pl.ds(pl.multiple_of(start, HEAD_SIZE), width)
@@ -310,30 +307,24 @@
     for n, (source, target) in enumerate(((k_hbm, k_own), (v_hbm, v_own))):
         loads.append(pltpu.make_async_copy(source, target, load_sem.at[n]))
         loads[-1].start()
-    own = []
-    for half in range(HALVES):
+    own, q_own = {}, {}
+    for half, n in PHASES:
         for kind, source in enumerate((k_hbm, v_hbm)):
-            item = 2 * half + kind
-            columns = lanes(kv_head(half, me) * HEAD_SIZE, HEAD_SIZE)
-            own.append(
-                pltpu.make_async_copy(
-                    source.at[:, columns],
-                    held[item].at[place_of(half, me, length)],
-                    own_sem.at[item],
-                )
+            item = (half * 2 + n) * 2 + kind
+            columns = lanes(kv_head(half, n, me) * HEAD_SIZE, HEAD_SIZE)
+            own[item] = pltpu.make_async_copy(
+                source.at[:, columns], held[item].at[place_of(half, me, length)], own_sem.at[item]
             )
-            own[-1].start()
-    q_own = []
-    for half in range(HALVES):
-        columns = lanes(kv_head(half, me) * per_kv, per_kv)
-        q_own.append(
-            pltpu.make_async_copy(q_hbm.at[:, columns], q_bufs[half][0], q_sem.at[half])
-        )
-        q_own[-1].start()
+            own[item].start()
+    for half, n in PHASES:
+        columns = lanes(kv_head(half, n, me) * per_kv, per_kv)
+        q_own[half, n] = pltpu.make_async_copy(
+            q_hbm.at[:, columns], q_bufs[half * 2 + n][0], q_sem.at[half * 2 + n]
+        )
+        q_own[half, n].start()
 
     barrier = pltpu.get_barrier_semaphore()
-    around = [relative(half, steps) for half in range(HALVES) for steps in NEAR]
-    around = around[:3] + around[4:]
+    around = [flipped(me, axis) for axis in ("x", "y", "core")]
     for where in around:
         pl.semaphore_signal(barrier, inc=1, device_id=device_at(where), device_id_type=MESH)
 
@@ -366,208 +357,225 @@
         sent.append(copy)
         return copy
 
-    exchanged = {}
-
-    def exchange(half):
+    exchanged, asked, answered, own_out = {}, {}, [], []
+
+    def exchange(half, n):
+        peer = partner(half)
+        columns = lanes(kv_head(half, n, peer) * HEAD_SIZE, HEAD_SIZE)
         for kind in range(2):
-            item = 2 * half + kind
-            for n, steps in enumerate(NEAR):
-                peer = relative(half, steps)
-                columns = lanes(kv_head(half, peer) * HEAD_SIZE, HEAD_SIZE)
-                exchanged[item, n] = begin(
-                    remote(
-                        sources[kind].at[:, columns],
-                        held[item].at[place_of(half, me, length)],
-                        ex_send.at[item, n],
-                        ex_recv.at[item, n],
-                        peer,
-                    )
-                )
-
-    asked = {}
-
-    def ask(half):
-        for n, steps in enumerate(NEAR):
-            peer = relative(half, steps)
-            columns = lanes(kv_head(half, peer) * per_kv, per_kv)
-            asked[half, n] = begin(
+            item = (half * 2 + n) * 2 + kind
+            exchanged[item] = begin(
                 remote(
-                    q_hbm.at[:, columns],
-                    q_bufs[half][n + 1],
-                    q_send.at[half, n],
-                    q_recv.at[half, n],
+                    sources[kind].at[:, columns],
+                    held[item].at[place_of(half, me, length)],
+                    ex_send.at[item],
+                    ex_recv.at[item],
                     peer,
                 )
             )
 
-    def hop(item, major, slab, way):
-        half = item // 2
-        _, other = axis_pair(half)
-        first = ((major * length + slab) * 2 + me[other]) * 2
-        part = held[item].at[pl.ds(first, 2)]
-        if way == 2:
-            where, lane = {**me, other: 1 - me[other]}, 1
+    def ask(half, n):
+        peer = partner(half)
+        columns = lanes(kv_head(half, n, peer) * per_kv, per_kv)
+        asked[half, n] = begin(
+            remote(
+                q_hbm.at[:, columns],
+                q_bufs[half * 2 + n][1],
+                q_send.at[half * 2 + n],
+                q_recv.at[half * 2 + n],
+                peer,
+            )
+        )
+
+    def part_of(item, core, slab, lane):
+        other = axis_pair(item // 4)[1]
+        side = me[other] if lane == 0 else 1 - me[other]
+        return held[item].at[pl.ds(((core * length + slab) * 2 + side) * 2, 2)]
+
+    def hop(item, slab, way):
+        other = axis_pair(item // 4)[1]
+        lane = 1 if way == BESIDE_TOO else 0
+        part = part_of(item, me["core"], slab, lane)
+        if way in (BESIDE, BESIDE_TOO):
+            where, recv = flipped(me, "core"), b_recv.at[item, slab, lane]
+        elif way == ACROSS:
+            where, recv = flipped(me, other), g_recv.at[item, slab, 1]
         else:
-            where, lane = {**me, "z": z + (1 if way == 0 else -1)}, 0
-        return remote(
-            part, part, g_send.at[item, major, slab, way], g_recv.at[item, major, slab, lane], where
-        )
-
-    def arrived(item, major, slab, lane):
-        half = item // 2
-        _, other = axis_pair(half)
-        side = me[other] if lane == 0 else 1 - me[other]
-        first = ((major * length + slab) * 2 + side) * 2
-        part = held[item].at[pl.ds(first, 2)]
-        remote(
-            part, part, g_send.at[item, major, slab, 0], g_recv.at[item, major, slab, lane], me
-        ).wait_recv()
-
-    def ways(item, kind):
-        up = (0, z < length - 1)
-        down = (1, z > 0)
-        across = (2, None if item >= 2 else me["x"] == 0)
-        return {"own": (up, down, across), "below": (up, across), "above": (down, across)}[kind]
-
-    def each_way(item, major, slab, kind, act):
-        for way, ok in ways(item, kind):
+            where, recv = {**me, "z": z + (1 if way == UP else -1)}, g_recv.at[item, slab, 0]
+        return remote(part, part, g_send.at[item, slab, way], recv, where)
+
+    def wait_for(item, slab, lane):
+        part = part_of(item, me["core"], slab, lane)
+        recv = g_recv.at[item, slab, lane]
+        remote(part, part, g_send.at[item, slab, 0], recv, me).wait_recv()
+
+    def wait_beside(item, slab, lane):
+        part = part_of(item, 1 - me["core"], slab, lane)
+        recv = b_recv.at[item, slab, lane]
+        remote(part, part, g_send.at[item, slab, 0], recv, me).wait_recv()
+
+    def each_way(item, slab, ways, act):
+        for way in ways:
+            ok = {
+                UP: z < length - 1,
+                DOWN: z > 0,
+                ACROSS: None if item >= 4 else me["x"] == 0,
+                BESIDE: None,
+                BESIDE_TOO: None,
+            }[way]
             if ok is None:
-                act(hop(item, major, slab, way))
+                act(hop(item, slab, way))
             else:
-                pl.when(ok)(lambda way=way: act(hop(item, major, slab, way)))
-
-    def start(item, major, slab, kind):
-        each_way(item, major, slab, kind, lambda copy: copy.start())
+                pl.when(ok)(lambda way=way: act(hop(item, slab, way)))
+
+    def started(copy):
+        copy.start()
+
+    def finished(copy):
+        copy.wait_send()
+
+    def visit(item, distance, act, wait=False):
+        if distance == 0:
+            each_way(item, z, (UP, DOWN, ACROSS, BESIDE), act)
+            return
+
+        @pl.when(z >= distance)
+        def _():
+            if wait:
+                wait_for(item, z - distance, 0)
+            each_way(item, z - distance, (UP, ACROSS, BESIDE), act)
+
+        @pl.when(z + distance < length)
+        def _():
+            if wait:
+                wait_for(item, z + distance, 0)
+            each_way(item, z + distance, (DOWN, ACROSS, BESIDE), act)
+
+    def crossed(item):
+        return lambda body: body() if item >= 4 else pl.when(me["x"] == 1)(body)
+
+    def items_of(phase):
+        half, n = PHASES[phase]
+        return [(half * 2 + n) * 2 + kind for kind in range(2)]
 
     def launch(item):
         own[item].wait()
-        for n in range(len(NEAR)):
-            exchanged[item, n].wait_recv()
-        for major in range(2):
-            start(item, major, z, "own")
-
-    def step(item, major, distance):
-        @pl.when(z >= distance)
+        exchanged[item].wait_recv()
+        visit(item, 0, started)
+
+    def step(item, distance):
+        if distance == 0:
+            launch(item)
+        else:
+            visit(item, distance, started, wait=True)
+
+    def steps(phase, distance):
+        return [(item, distance) for item in items_of(phase)]
+
+    def settle(phase):
+        for item in items_of(phase):
+            @crossed(item)
+            def _():
+                for slab in range(length):
+                    wait_for(item, slab, 1)
+                    each_way(item, slab, (BESIDE_TOO,), started)
+
+        for item in items_of(phase):
+            for slab in range(length):
+                wait_beside(item, slab, 0)
+
+            @crossed(item)
+            def _():
+                for slab in range(length):
+                    wait_beside(item, slab, 1)
+
+        q_own[PHASES[phase]].wait()
+        asked[PHASES[phase]].wait_recv()
+
+    def drain(item):
+        for distance in range(length):
+            visit(item, distance, finished)
+
+        @crossed(item)
         def _():
-            arrived(item, major, z - distance, 0)
-            start(item, major, z - distance, "below")
-
-        @pl.when(z + distance < length)
-        def _():
-            arrived(item, major, z + distance, 0)
-            start(item, major, z + distance, "above")
-
-    def settle(item):
-        def crossing():
-            for major in range(2):
-                for slab in range(length):
-                    arrived(item, major, slab, 1)
-
-        if item >= 2:
-            crossing()
-        else:
-            pl.when(me["x"] == 1)(crossing)
-
-    def drain(item):
-        for major in range(2):
-            each_way(item, major, z, "own", lambda copy: copy.wait_send())
-            for distance in range(1, length):
-                @pl.when(z >= distance)
-                def _():
-                    each_way(
-                        item, major, z - distance, "below", lambda copy: copy.wait_send()
-                    )
-
-                @pl.when(z + distance < length)
-                def _():
-                    each_way(
-                        item, major, z + distance, "above", lambda copy: copy.wait_send()
-                    )
-
-    answered = []
-
-    def answer(half, turn):
-        columns = lanes(kv_head(half, me) * per_kv + turn * HEAD_SIZE, HEAD_SIZE)
-        local = pl.ds(turn * HEAD_SIZE, HEAD_SIZE)
-        for n, steps in enumerate(NEAR):
-            copy = begin(
-                remote(
-                    o_bufs[half][n + 1].at[:, local],
-                    out_hbm.at[:, columns],
-                    o_send.at[half, turn, n],
-                    o_recv.at[half, turn, n],
-                    relative(half, steps),
-                )
+            for slab in range(length):
+                each_way(item, slab, (BESIDE_TOO,), finished)
+
+    def answer(phase, gang):
+        half, n = PHASES[phase]
+        index = half * 2 + n
+        width = GANG * HEAD_SIZE
+        columns = lanes(kv_head(half, n, me) * per_kv + gang * width, width)
+        local = pl.ds(gang * width, width)
+        copy = begin(
+            remote(
+                o_bufs[index][1].at[:, local],
+                out_hbm.at[:, columns],
+                o_send.at[index, gang],
+                o_recv.at[index, gang],
+                partner(half),
             )
-            answered.append(copy)
+        )
+        answered.append(copy)
         copy = pltpu.make_async_copy(
-            o_bufs[half][0].at[:, local], out_hbm.at[:, columns], o_sem.at[half, turn]
+            o_bufs[index][0].at[:, local], out_hbm.at[:, columns], o_sem.at[index, gang]
         )
         copy.start()
         own_out.append(copy)
 
-    own_out = []
-    where_from = ((0, 0),) + NEAR
-
-    def compute(half, turn):
-        places = [block_at(relative(half, steps)) for steps in where_from]
-        attend(
-            half,
-            q_bufs[half],
-            held[2 * half],
-            held[2 * half + 1],
-            place_ref,
-            vert_ref,
-            slash_ref,
-            o_bufs[half],
-            kv_head(half, me) * turns + turn,
-            turn,
-            places,
-        )
-        answer(half, turn)
-
-    def steps_of(half, distance):
-        return [(2 * half + kind, major, distance) for kind in range(2) for major in range(2)]
-
-    exchange(0)
-    exchange(1)
-    ask(0)
-    launch(0)
-    launch(1)
-    for distance in range(1, length - 1):
-        for args in steps_of(0, distance):
-            step(*args)
-    launch(2)
-    launch(3)
-    for args in steps_of(0, length - 1):
-        step(*args)
-    ask(1)
-    pending = [args for distance in range(1, length) for args in steps_of(1, distance)]
-    for args in pending[:2]:
-        step(*args)
-    pending = pending[2:]
-    settle(0)
-    settle(1)
-    q_own[0].wait()
-    for n in range(len(NEAR)):
-        asked[0, n].wait_recv()
-    for turn in range(turns):
-        compute(0, turn)
-        for args in pending[:1]:
-            step(*args)
-        pending = pending[1:]
-    for args in pending:
-        step(*args)
-    settle(2)
-    settle(3)
-    q_own[1].wait()
-    for n in range(len(NEAR)):
-        asked[1, n].wait_recv()
-    for turn in range(turns):
-        compute(1, turn)
+    def compute(phase, gang):
+        half, n = PHASES[phase]
+        index = half * 2 + n
+        units = []
+        for turn in range(gang * GANG, (gang + 1) * GANG):
+            for side, where in enumerate((me, partner(half))):
+                units.append(
+                    (
+                        q_bufs[index][side],
+                        o_bufs[index][side],
+                        pl.ds(turn * HEAD_SIZE, HEAD_SIZE),
+                        kv_head(half, n, me) * turns + turn,
+                        block_at(where),
+                    )
+                )
+        k_item, v_item = items_of(phase)
+        attend(half, units, held[k_item], held[v_item], place_ref, vert_ref, slash_ref)
+
+    def run(todo):
+        for item, distance in todo:
+            step(item, distance)
+
+    for phase in range(4):
+        exchange(*PHASES[phase])
+    ask(0, 0)
+    ask(0, 1)
+    run(steps(0, 0) + steps(0, 1))
+    run(steps(1, 0) + steps(0, 2) + steps(1, 1) + steps(0, 3))
+    ask(1, 0)
+    run(steps(2, 0) + steps(1, 2) + steps(2, 1) + steps(1, 3))
+    later = [
+        steps(3, 0) + steps(2, 2) + steps(3, 1)[:1],
+        steps(3, 1)[1:] + steps(2, 3) + steps(3, 2)[:1],
+        steps(3, 2)[1:] + steps(3, 3),
+    ]
+    for phase in range(4):
+        settle(phase)
+        todo = later[phase] if phase < 3 else []
+        if phase == 2:
+            ask(1, 1)
+        for gang in range(gangs):
+            compute(phase, gang)
+            share = -(-len(todo) // (gangs - gang))
+            run(todo[:share])
+            todo = todo[share:]
+            if phase != 2:
+                answer(phase, gang)
+        if phase == 2:
+            for gang in range(gangs):
+                answer(phase, gang)
     for copy in sent:
         copy.wait_send()
-    for item in range(4):
+    for item in range(8):
         drain(item)
     for copy in answered:
         copy.wait_recv()
@@ -580,7 +588,6 @@
     blocks = group_count * uly_count
     length = uly_count // 2
     turns = QUERY_HEADS // KEY_VALUE_HEADS
-    near = len(NEAR)
     dtype = queries.dtype
     smem = pl.BlockSpec(memory_space=pltpu.SMEM)
     hbm = pl.BlockSpec(memory_space=pl.ANY)
@@ -595,20 +602,21 @@
             pltpu.VMEM(key_state_rows.shape, dtype),
             pltpu.VMEM(value_state_rows.shape, dtype),
             dma((2,)),
+            dma((8,)),
+            dma((8,)),
+            dma((8,)),
             dma((4,)),
-            dma((4, near)),
-            dma((4, near)),
-            dma((HALVES,)),
-            dma((HALVES, near)),
-            dma((HALVES, near)),
-            dma((4, 2, length, 3)),
-            dma((4, 2, length, 2)),
-            dma((HALVES, turns)),
-            dma((HALVES, turns, near)),
-            dma((HALVES, turns, near)),
+            dma((4,)),
+            dma((4,)),
+            dma((8, length, 5)),
+            dma((8, length, 2)),
+            dma((8, length, 2)),
+            dma((4, turns // GANG)),
+            dma((4, turns // GANG)),
+            dma((4, turns // GANG)),
         ]
-        + [pltpu.VMEM((blocks, BLOCK_TOKENS, HEAD_SIZE), dtype)] * 4
-        + [pltpu.VMEM(share, dtype)] * (4 * HALVES * 2),
+        + [pltpu.VMEM((blocks, BLOCK_TOKENS, HEAD_SIZE), dtype)] * 8
+        + [pltpu.VMEM(share, dtype)] * 16,
         compiler_params=pltpu.CompilerParams(collective_id=0, has_side_effects=True),
         name="split_and_attend",
     )(
@@ -624,9 +632,9 @@
 def chosen(queries, key_state_rows, *rest):
     group_count, uly_count = lax.axis_size("grp"), lax.axis_size("uly")
     fits = (
-        group_count == FOUR
-        and uly_count == 2 * FOUR
-        and KEY_VALUE_HEADS == HALVES * FOUR
+        group_count == 4
+        and uly_count == 8
+        and KEY_VALUE_HEADS == 4 * HALVES
         and queries.shape[0] == BLOCK_TOKENS
     )
     plan = split_shards if fits else shards

time: 81 us -> 71.4 us (0.88)
  Pallas kernels: 77.7 us -> 68.1 us
    pallas_call x1, Pallas kernels: 77.7 us -> 68.1 us  [split_shards(): pl.pallas_call(functools.partial(split_kernel, uly_count), out_shape=jax....]
where the time goes in v2:
time: 71.4 us; the launch traced here: 71.3 us
  Pallas kernels  68.1 us (95%)
  local copies, waits for them, and re-layouts  3.1 us (4%)
    pallas_call x1, Pallas kernels, split_shards(): pl.pallas_call(functools.partial(split_kernel, uly_count), out_shape=jax....  68.1 us
    unnamed x1, local copies, waits for them, and re-layouts  3.1 us

profile of v2, /device:TPU:0, one launch (start us, length us, event | category | flops | bytes accessed | tf_op | source)
XLA Modules:
  0.0 71.3 jit_solution(866112850194975591)
XLA Ops:
  0.0 68.1 %split_and_attend.1 = bf16[128,8192]{1,0:T(8,128)(2,1)} custom-call(s32[2,32]{1,0:T(2,128)} %constant.2.clone.place_ref, s32[6,64]{1,0:T(8,128)} %bitcast.2, s32[3,64]{1,0:T(4,128)} %bitcast.3, bf16[128,8192]{1,0:T(8,128)(2,1)} %q_hbm.1, bf16[128,1024]{1,0:T(8,128)(2,1)} %k_hbm.1, bf16[128,1024]{1,0:T(8,128)(2,1)} %v_hbm.1), custom_call_target="tpu_custom_call" | custom-call | tf_op jit(solution)/shard_map/split_and_attend/pallas_call | solution.py:596
  68.2 3.1 %copy.8 = bf16[128,8192]{1,0:T(8,128)(2,1)} copy(bf16[128,8192]{1,0:T(8,128)(2,1)} %split_and_attend.1) | data formatting | bytes 4194304

commit v3 on v2

--- a/solution.py
+++ b/solution.py
@@ -164,8 +164,10 @@
 MESH = pl.DeviceIdType.MESH
 LOG2_E = 1.4426950408889634
 HALVES = 2
-PHASES = ((0, 0), (1, 0), (0, 1), (1, 1))
-UP, DOWN, ACROSS, BESIDE, BESIDE_TOO = range(5)
+PHASES = ((1, 0), (0, 0), (1, 1), (0, 1))
+UP, DOWN, ACROSS, BESIDE, UP_TOO, DOWN_TOO, BESIDE_TOO = range(7)
+WIDE_FIRST = ()
+EAGER = True
 GANG = 2
 
 
@@ -258,7 +260,7 @@
     q_hbm,
     k_hbm,
     v_hbm,
-    out_hbm,
+    out_ref,
     k_own,
     v_own,
     load_sem,
@@ -392,16 +394,18 @@
         side = me[other] if lane == 0 else 1 - me[other]
         return held[item].at[pl.ds(((core * length + slab) * 2 + side) * 2, 2)]
 
-    def hop(item, slab, way):
+    def hop(item, slab, way, part=None):
         other = axis_pair(item // 4)[1]
-        lane = 1 if way == BESIDE_TOO else 0
-        part = part_of(item, me["core"], slab, lane)
+        lane = 1 if way in (UP_TOO, DOWN_TOO, BESIDE_TOO) else 0
+        if part is None:
+            part = part_of(item, me["core"], slab, lane)
         if way in (BESIDE, BESIDE_TOO):
             where, recv = flipped(me, "core"), b_recv.at[item, slab, lane]
         elif way == ACROSS:
             where, recv = flipped(me, other), g_recv.at[item, slab, 1]
         else:
-            where, recv = {**me, "z": z + (1 if way == UP else -1)}, g_recv.at[item, slab, 0]
+            where = {**me, "z": z + (1 if way in (UP, UP_TOO) else -1)}
+            recv = g_recv.at[item, slab, lane]
         return remote(part, part, g_send.at[item, slab, way], recv, where)
 
     def wait_for(item, slab, lane):
@@ -414,19 +418,20 @@
         recv = b_recv.at[item, slab, lane]
         remote(part, part, g_send.at[item, slab, 0], recv, me).wait_recv()
 
-    def each_way(item, slab, ways, act):
+    def each_way(item, slab, ways, act, part=None):
         for way in ways:
-            ok = {
-                UP: z < length - 1,
-                DOWN: z > 0,
-                ACROSS: None if item >= 4 else me["x"] == 0,
-                BESIDE: None,
-                BESIDE_TOO: None,
-            }[way]
+            if way in (UP, UP_TOO):
+                ok = z < length - 1
+            elif way in (DOWN, DOWN_TOO):
+                ok = z > 0
+            elif way == ACROSS and item < 4:
+                ok = me["x"] == 0
+            else:
+                ok = None
             if ok is None:
-                act(hop(item, slab, way))
+                act(hop(item, slab, way, part))
             else:
-                pl.when(ok)(lambda way=way: act(hop(item, slab, way)))
+                pl.when(ok)(lambda way=way: act(hop(item, slab, way, part)))
 
     def started(copy):
         copy.start()
@@ -435,21 +440,47 @@
         copy.wait_send()
 
     def visit(item, distance, act, wait=False):
+        first = item in WIDE_FIRST
         if distance == 0:
             each_way(item, z, (UP, DOWN, ACROSS, BESIDE), act)
             return
+        across = () if first else (ACROSS,)
 
         @pl.when(z >= distance)
         def _():
             if wait:
                 wait_for(item, z - distance, 0)
-            each_way(item, z - distance, (UP, ACROSS, BESIDE), act)
+            each_way(item, z - distance, (UP,) + across + (BESIDE,), act)
 
         @pl.when(z + distance < length)
         def _():
             if wait:
                 wait_for(item, z + distance, 0)
-            each_way(item, z + distance, (DOWN, ACROSS, BESIDE), act)
+            each_way(item, z + distance, (DOWN,) + across + (BESIDE,), act)
+
+        if first:
+            visit_too(item, distance, act, wait)
+
+    def visit_too(item, distance, act, wait=False):
+        @crossed(item)
+        def _():
+            if distance == 0:
+                if wait:
+                    wait_for(item, z, 1)
+                each_way(item, z, (UP_TOO, DOWN_TOO, BESIDE_TOO), act)
+                return
+
+            @pl.when(z >= distance)
+            def _():
+                if wait:
+                    wait_for(item, z - distance, 1)
+                each_way(item, z - distance, (UP_TOO, BESIDE_TOO), act)
+
+            @pl.when(z + distance < length)
+            def _():
+                if wait:
+                    wait_for(item, z + distance, 1)
+                each_way(item, z + distance, (DOWN_TOO, BESIDE_TOO), act)
 
     def crossed(item):
         return lambda body: body() if item >= 4 else pl.when(me["x"] == 1)(body)
@@ -463,19 +494,36 @@
         exchanged[item].wait_recv()
         visit(item, 0, started)
 
+    def launch_early(item, mine):
+        half = item // 4
+        where = me if mine else partner(half)
+        if mine:
+            own[item].wait()
+        else:
+            exchanged[item].wait_recv()
+        block = held[item].at[pl.ds(place_of(half, where, length), 1)]
+        each_way(item, z, (UP, DOWN, ACROSS, BESIDE), started, block)
+
     def step(item, distance):
         if distance == 0:
             launch(item)
+        elif distance == "too":
+            visit_too(item, 0, started, wait=True)
         else:
             visit(item, distance, started, wait=True)
 
     def steps(phase, distance):
-        return [(item, distance) for item in items_of(phase)]
+        todo = [(item, distance) for item in items_of(phase)]
+        if distance == 0:
+            todo += [(item, "too") for item in items_of(phase) if item in WIDE_FIRST]
+        return todo
 
     def settle(phase):
         for item in items_of(phase):
             @crossed(item)
             def _():
+                if item in WIDE_FIRST:
+                    return
                 for slab in range(length):
                     wait_for(item, slab, 1)
                     each_way(item, slab, (BESIDE_TOO,), started)
@@ -495,6 +543,10 @@
     def drain(item):
         for distance in range(length):
             visit(item, distance, finished)
+
+        if item in WIDE_FIRST:
+            visit_too(item, 0, finished)
+            return
 
         @crossed(item)
         def _():
@@ -510,7 +562,7 @@
         copy = begin(
             remote(
                 o_bufs[index][1].at[:, local],
-                out_hbm.at[:, columns],
+                out_ref.at[:, columns],
                 o_send.at[index, gang],
                 o_recv.at[index, gang],
                 partner(half),
@@ -518,7 +570,7 @@
         )
         answered.append(copy)
         copy = pltpu.make_async_copy(
-            o_bufs[index][0].at[:, local], out_hbm.at[:, columns], o_sem.at[index, gang]
+            o_bufs[index][0].at[:, local], out_ref.at[:, columns], o_sem.at[index, gang]
         )
         copy.start()
         own_out.append(copy)
@@ -547,11 +599,17 @@
 
     for phase in range(4):
         exchange(*PHASES[phase])
-    ask(0, 0)
-    ask(0, 1)
-    run(steps(0, 0) + steps(0, 1))
+    ask(*PHASES[0])
+    ask(*PHASES[2])
+    if EAGER:
+        for mine in (True, False):
+            for item in items_of(0):
+                launch_early(item, mine)
+        run(steps(0, 0)[2:] + steps(0, 1))
+    else:
+        run(steps(0, 0) + steps(0, 1))
     run(steps(1, 0) + steps(0, 2) + steps(1, 1) + steps(0, 3))
-    ask(1, 0)
+    ask(*PHASES[1])
     run(steps(2, 0) + steps(1, 2) + steps(2, 1) + steps(1, 3))
     later = [
         steps(3, 0) + steps(2, 2) + steps(3, 1)[:1],
@@ -562,7 +620,7 @@
         settle(phase)
         todo = later[phase] if phase < 3 else []
         if phase == 2:
-            ask(1, 1)
+            ask(*PHASES[3])
         for gang in range(gangs):
             compute(phase, gang)
             share = -(-len(todo) // (gangs - gang))
@@ -595,9 +653,9 @@
     share = (BLOCK_TOKENS, turns * HEAD_SIZE)
     return pl.pallas_call(
         functools.partial(split_kernel, uly_count),
-        out_shape=jax.ShapeDtypeStruct(queries.shape, dtype),
+        out_shape=pltpu.VMEM(queries.shape, dtype),
         in_specs=[smem, smem, smem, hbm, hbm, hbm],
-        out_specs=hbm,
+        out_specs=pl.BlockSpec(memory_space=pltpu.VMEM),
         scratch_shapes=[
             pltpu.VMEM(key_state_rows.shape, dtype),
             pltpu.VMEM(value_state_rows.shape, dtype),
@@ -608,7 +666,7 @@
             dma((4,)),
             dma((4,)),
             dma((4,)),
-            dma((8, length, 5)),
+            dma((8, length, 7)),
             dma((8, length, 2)),
             dma((8, length, 2)),
             dma((4, turns // GANG)),

time: 71.4 us -> 69.1 us (0.968); the launches traced: 71.3 us -> 67.8 us
  local copies, waits for them, and re-layouts: 3.1 us -> 1.32 us
  Pallas kernels: 68.1 us -> 66.5 us
    unnamed x1, local copies, waits for them, and re-layouts: 3.1 us -> 1.32 us
    pallas_call x1, Pallas kernels: 68.1 us -> 66.5 us  [split_shards(): pl.pallas_call(functools.partial(split_kernel, uly_count), out_shape=pltp...]
where the time goes in v3:
time: 69.1 us; the launch traced here: 67.8 us
  Pallas kernels  66.5 us (96%)
  local copies, waits for them, and re-layouts  1.32 us (2%)
    pallas_call x1, Pallas kernels, split_shards(): pl.pallas_call(functools.partial(split_kernel, uly_count), out_shape=pltp...  66.5 us

profile of v3, /device:TPU:0, one launch (start us, length us, event | category | flops | bytes accessed | tf_op | source)
XLA Modules:
  0.0 67.8 jit_solution(11716705820265128783)
XLA Ops:
  0.0 66.5 %split_and_attend.1 = bf16[128,8192]{1,0:T(8,128)(2,1)S(1)} custom-call(s32[2,32]{1,0:T(2,128)} %constant.2.clone.place_ref, s32[6,64]{1,0:T(8,128)} %bitcast.2, s32[3,64]{1,0:T(4,128)} %bitcast.3, bf16[128,8192]{1,0:T(8,128)(2,1)} %q_hbm.1, bf16[128,1024]{1,0:T(8,128)(2,1)} %k_hbm.1, bf16[128,1024]{1,0:T(8,128)(2,1)} %v_hbm.1), custom_call_target="tpu_custom_call" | custom-call | tf_op jit(solution)/shard_map/split_and_attend/pallas_call | solution.py:654
  66.5 1.3 %copy.8 = bf16[128,8192]{1,0:T(8,128)(2,1)} copy(bf16[128,8192]{1,0:T(8,128)(2,1)S(1)} %split_and_attend.1) | data formatting | bytes 4194304

commit v4 on v3

--- a/solution.py
+++ b/solution.py
@@ -166,8 +166,7 @@
 HALVES = 2
 PHASES = ((1, 0), (0, 0), (1, 1), (0, 1))
 UP, DOWN, ACROSS, BESIDE, UP_TOO, DOWN_TOO, BESIDE_TOO = range(7)
-WIDE_FIRST = ()
-EAGER = True
+SHORT = ()
 GANG = 2
 
 
@@ -188,40 +187,15 @@
     return ((where["core"] * length + where["z"]) * 2 + where[other]) * 2 + where[shared]
 
 
-def place_table(group_count, uly_count):
-    block = np.arange(group_count * uly_count)
-    where = whereabouts(block // uly_count, block % uly_count)
-    rows = [place_of(half, where, uly_count // 2) for half in range(HALVES)]
-    return np.stack(rows).astype(np.int32)
-
-
-def attend(row, units, k_buf, v_buf, place_ref, vert_ref, slash_ref):
-    slash_slots, vert_slots = slash_ref.shape[0], vert_ref.shape[0]
+def attend(units, k_buf, v_buf, table_ref, bias_ref):
+    slots = range(table_ref.shape[1])
     rate = HEAD_SIZE ** (-0.5) * LOG2_E
     causal = lax.broadcasted_iota(
         jnp.int32, (BLOCK_TOKENS, BLOCK_TOKENS), 0
     ) >= lax.broadcasted_iota(jnp.int32, (BLOCK_TOKENS, BLOCK_TOKENS), 1)
-
-    def slots_of(q_head, here):
-        blocks, allowed = [here], [None]
-        offsets = [slash_ref[slot, q_head] for slot in range(slash_slots)]
-        for offset in offsets:
-            ok = (offset >= 1) & (here - offset >= 0)
-            blocks.append(jnp.where(ok, here - offset, here))
-            allowed.append(ok)
-        for slot in range(vert_slots):
-            block = vert_ref[slot, q_head]
-            ok = (block >= 0) & (block < here)
-            for offset in offsets:
-                ok = ok & jnp.logical_not((offset >= 1) & (here - offset == block))
-            blocks.append(jnp.where(ok, block, here))
-            allowed.append(ok)
-        return blocks, allowed
-
-    chosen_slots = [slots_of(q_head, here) for _, _, _, q_head, here in units]
     scores, probs, totals = [], [], []
-    for (q_ref, _, columns, _, _), (blocks, _) in zip(units, chosen_slots):
-        keys = jnp.concatenate([k_buf[place_ref[row, block]] for block in blocks], axis=0)
+    for q_ref, _, columns, line in units:
+        keys = jnp.concatenate([k_buf[table_ref[line, slot]] for slot in slots], axis=0)
         scores.append(
             lax.dot_general(
                 q_ref[:, columns],
@@ -230,37 +204,39 @@
                 preferred_element_type=jnp.float32,
             )
         )
-    for score, (_, allowed) in zip(scores, chosen_slots):
+    for score, (_, _, _, line) in zip(scores, units):
         pieces = []
-        for slot, ok in enumerate(allowed):
+        for slot in slots:
             piece = score[:, slot * BLOCK_TOKENS : (slot + 1) * BLOCK_TOKENS]
-            if ok is None:
+            if slot == 0:
                 pieces.append(jnp.where(causal, piece, neg_large))
             else:
-                pieces.append(piece + jnp.where(ok, 0.0, neg_large).astype(jnp.float32))
+                pieces.append(piece + bias_ref[line, slot])
         best = functools.reduce(jnp.maximum, pieces)
         best = jnp.max(best, axis=1, keepdims=True)
         weights = [jnp.exp2((piece - best) * rate) for piece in pieces]
         total = functools.reduce(jnp.add, weights)
         totals.append(jnp.sum(total, axis=1, keepdims=True))
         probs.append(jnp.concatenate([weight.astype(jnp.bfloat16) for weight in weights], axis=1))
-    for (_, o_ref, columns, _, _), prob, total, (blocks, _) in zip(
-        units, probs, totals, chosen_slots
-    ):
-        values = jnp.concatenate([v_buf[place_ref[row, block]] for block in blocks], axis=0)
+    for (_, o_ref, columns, line), prob, total in zip(units, probs, totals):
+        values = jnp.concatenate([v_buf[table_ref[line, slot]] for slot in slots], axis=0)
         mixed = jnp.dot(prob, values, preferred_element_type=jnp.float32)
         o_ref[:, columns] = (mixed / total).astype(o_ref.dtype)
 
 
 def split_kernel(
     uly_count,
-    place_ref,
-    vert_ref,
-    slash_ref,
+    vert_hbm,
+    slash_hbm,
     q_hbm,
     k_hbm,
     v_hbm,
     out_ref,
+    vert_ref,
+    slash_ref,
+    list_sem,
+    table_ref,
+    bias_ref,
     k_own,
     v_own,
     load_sem,
@@ -305,6 +281,10 @@
     def lanes(start, width):
         return pl.ds(pl.multiple_of(start, HEAD_SIZE), width)
 
+    lists = []
+    for n, (source, target) in enumerate(((vert_hbm, vert_ref), (slash_hbm, slash_ref))):
+        lists.append(pltpu.make_async_copy(source, target, list_sem.at[n]))
+        lists[-1].start()
     loads = []
     for n, (source, target) in enumerate(((k_hbm, k_own), (v_hbm, v_own))):
         loads.append(pltpu.make_async_copy(source, target, load_sem.at[n]))
@@ -440,11 +420,10 @@
         copy.wait_send()
 
     def visit(item, distance, act, wait=False):
-        first = item in WIDE_FIRST
         if distance == 0:
             each_way(item, z, (UP, DOWN, ACROSS, BESIDE), act)
             return
-        across = () if first else (ACROSS,)
+        across = () if item in SHORT and distance == 1 else (ACROSS,)
 
         @pl.when(z >= distance)
         def _():
@@ -458,29 +437,23 @@
                 wait_for(item, z + distance, 0)
             each_way(item, z + distance, (DOWN,) + across + (BESIDE,), act)
 
-        if first:
-            visit_too(item, distance, act, wait)
-
     def visit_too(item, distance, act, wait=False):
+        ways = (UP_TOO, DOWN_TOO, BESIDE_TOO) if distance == 0 and item in SHORT else (BESIDE_TOO,)
+
         @crossed(item)
         def _():
-            if distance == 0:
-                if wait:
-                    wait_for(item, z, 1)
-                each_way(item, z, (UP_TOO, DOWN_TOO, BESIDE_TOO), act)
-                return
-
             @pl.when(z >= distance)
             def _():
                 if wait:
                     wait_for(item, z - distance, 1)
-                each_way(item, z - distance, (UP_TOO, BESIDE_TOO), act)
-
-            @pl.when(z + distance < length)
-            def _():
-                if wait:
-                    wait_for(item, z + distance, 1)
-                each_way(item, z + distance, (DOWN_TOO, BESIDE_TOO), act)
+                each_way(item, z - distance, ways, act)
+
+            if distance:
+                @pl.when(z + distance < length)
+                def _():
+                    if wait:
+                        wait_for(item, z + distance, 1)
+                    each_way(item, z + distance, ways, act)
 
     def crossed(item):
         return lambda body: body() if item >= 4 else pl.when(me["x"] == 1)(body)
@@ -507,27 +480,24 @@
     def step(item, distance):
         if distance == 0:
             launch(item)
-        elif distance == "too":
-            visit_too(item, 0, started, wait=True)
+        elif distance < 0:
+            visit_too(item, -1 - distance, started, wait=True)
         else:
             visit(item, distance, started, wait=True)
 
     def steps(phase, distance):
         todo = [(item, distance) for item in items_of(phase)]
-        if distance == 0:
-            todo += [(item, "too") for item in items_of(phase) if item in WIDE_FIRST]
+        short = [item for item in items_of(phase) if item in SHORT]
+        if distance == 1:
+            todo += [(item, -1) for item in short]
+        if distance == length - 1:
+            todo += [(item, -2) for item in short]
         return todo
 
     def settle(phase):
         for item in items_of(phase):
-            @crossed(item)
-            def _():
-                if item in WIDE_FIRST:
-                    return
-                for slab in range(length):
-                    wait_for(item, slab, 1)
-                    each_way(item, slab, (BESIDE_TOO,), started)
-
+            for distance in range(2 if item in SHORT else 0, length):
+                visit_too(item, distance, started, wait=True)
         for item in items_of(phase):
             for slab in range(length):
                 wait_beside(item, slab, 0)
@@ -543,15 +513,7 @@
     def drain(item):
         for distance in range(length):
             visit(item, distance, finished)
-
-        if item in WIDE_FIRST:
-            visit_too(item, 0, finished)
-            return
-
-        @crossed(item)
-        def _():
-            for slab in range(length):
-                each_way(item, slab, (BESIDE_TOO,), finished)
+            visit_too(item, distance, finished)
 
     def answer(phase, gang):
         half, n = PHASES[phase]
@@ -580,18 +542,60 @@
         index = half * 2 + n
         units = []
         for turn in range(gang * GANG, (gang + 1) * GANG):
-            for side, where in enumerate((me, partner(half))):
+            for side in range(2):
                 units.append(
                     (
                         q_bufs[index][side],
                         o_bufs[index][side],
                         pl.ds(turn * HEAD_SIZE, HEAD_SIZE),
-                        kv_head(half, n, me) * turns + turn,
-                        block_at(where),
+                        (phase * turns + turn) * 2 + side,
                     )
                 )
         k_item, v_item = items_of(phase)
-        attend(half, units, held[k_item], held[v_item], place_ref, vert_ref, slash_ref)
+        attend(units, held[k_item], held[v_item], table_ref, bias_ref)
+
+    def tabulate(phase):
+        half, n = PHASES[phase]
+        first = kv_head(half, n, me) * turns
+        if phase == 0:
+            for copy in lists:
+                copy.wait()
+
+        def place_at(block):
+            group, member = lax.div(block, uly_count), lax.rem(block, uly_count)
+            where = {
+                "x": lax.div(group, 2),
+                "core": lax.rem(group, 2),
+                "y": lax.rem(member, 2),
+                "z": lax.div(member, 2),
+            }
+            return place_of(half, where, length)
+
+        @pl.loop(0, turns)
+        def _(turn):
+            q_head = first + turn
+            offsets = [slash_ref[slot, q_head] for slot in range(slash_ref.shape[0])]
+            listed = [vert_ref[slot, q_head] for slot in range(vert_ref.shape[0])]
+            for side, where in enumerate((me, partner(half))):
+                line = (phase * turns + turn) * 2 + side
+                here = block_at(where)
+                rows = [(here, None)]
+                targets = []
+                for offset in offsets:
+                    ok = (offset >= 1) & (here - offset >= 0)
+                    targets.append(jnp.where(ok, here - offset, -1))
+                    rows.append((here - offset, ok))
+                for block in listed:
+                    ok = (block >= 0) & (block < here)
+                    for target in targets:
+                        ok = ok & (block != target)
+                    rows.append((block, ok))
+                for slot, (block, ok) in enumerate(rows):
+                    if ok is None:
+                        table_ref[line, slot] = place_at(block)
+                    else:
+                        table_ref[line, slot] = place_at(jnp.where(ok, block, here))
+                        bias_ref[line, slot] = jnp.where(ok, 0.0, neg_large).astype(jnp.float32)
 
     def run(todo):
         for item, distance in todo:
@@ -600,37 +604,39 @@
     for phase in range(4):
         exchange(*PHASES[phase])
     ask(*PHASES[0])
+    for mine in (True, False):
+        for item in items_of(0):
+            launch_early(item, mine)
+    tabulate(0)
+    run(steps(0, 1) + steps(1, 0))
+    tabulate(1)
+    run(steps(0, 2))
+    tabulate(2)
+    run(steps(1, 1) + steps(0, 3))
+    ask(*PHASES[1])
+    tabulate(3)
+    run(steps(2, 0) + steps(1, 2) + steps(2, 1) + steps(1, 3))
     ask(*PHASES[2])
-    if EAGER:
-        for mine in (True, False):
-            for item in items_of(0):
-                launch_early(item, mine)
-        run(steps(0, 0)[2:] + steps(0, 1))
-    else:
-        run(steps(0, 0) + steps(0, 1))
-    run(steps(1, 0) + steps(0, 2) + steps(1, 1) + steps(0, 3))
-    ask(*PHASES[1])
-    run(steps(2, 0) + steps(1, 2) + steps(2, 1) + steps(1, 3))
-    later = [
-        steps(3, 0) + steps(2, 2) + steps(3, 1)[:1],
-        steps(3, 1)[1:] + steps(2, 3) + steps(3, 2)[:1],
-        steps(3, 2)[1:] + steps(3, 3),
-    ]
+    run(steps(3, 0))
+    between = (
+        ((), (), steps(2, 2)[:1], steps(2, 2)[1:]),
+        (steps(3, 1)[:1], steps(3, 1)[1:], steps(2, 3)[:1], steps(2, 3)[1:] + steps(3, 2)),
+        ((), steps(3, 3)[:1], steps(3, 3)[1:], ()),
+        ((), (), (), ()),
+    )
+    held_back = {0: (0,), 1: (1,), 2: (2,)}
     for phase in range(4):
         settle(phase)
-        todo = later[phase] if phase < 3 else []
-        if phase == 2:
-            ask(*PHASES[3])
         for gang in range(gangs):
             compute(phase, gang)
-            share = -(-len(todo) // (gangs - gang))
-            run(todo[:share])
-            todo = todo[share:]
-            if phase != 2:
+            run(between[phase][gang])
+            if phase == 3:
                 answer(phase, gang)
-        if phase == 2:
+        if phase == 1:
+            ask(*PHASES[3])
+        for ready in held_back.get(phase, ()):
             for gang in range(gangs):
-                answer(phase, gang)
+                answer(ready, gang)
     for copy in sent:
         copy.wait_send()
     for item in range(8):
@@ -646,17 +652,22 @@
     blocks = group_count * uly_count
     length = uly_count // 2
     turns = QUERY_HEADS // KEY_VALUE_HEADS
+    slots = 1 + slash_offsets.shape[1] + vert_blocks.shape[1]
     dtype = queries.dtype
-    smem = pl.BlockSpec(memory_space=pltpu.SMEM)
     hbm = pl.BlockSpec(memory_space=pl.ANY)
     dma = pltpu.SemaphoreType.DMA
     share = (BLOCK_TOKENS, turns * HEAD_SIZE)
     return pl.pallas_call(
         functools.partial(split_kernel, uly_count),
         out_shape=pltpu.VMEM(queries.shape, dtype),
-        in_specs=[smem, smem, smem, hbm, hbm, hbm],
+        in_specs=[hbm] * 5,
         out_specs=pl.BlockSpec(memory_space=pltpu.VMEM),
         scratch_shapes=[
+            pltpu.SMEM(vert_blocks.shape[::-1], jnp.int32),
+            pltpu.SMEM(slash_offsets.shape[::-1], jnp.int32),
+            dma((2,)),
+            pltpu.SMEM((8 * turns, slots), jnp.int32),
+            pltpu.SMEM((8 * turns, slots), jnp.float32),
             pltpu.VMEM(key_state_rows.shape, dtype),
             pltpu.VMEM(value_state_rows.shape, dtype),
             dma((2,)),
@@ -678,7 +689,6 @@
         compiler_params=pltpu.CompilerParams(collective_id=0, has_side_effects=True),
         name="split_and_attend",
     )(
-        jnp.asarray(place_table(group_count, uly_count)),
         vert_blocks.T,
         slash_offsets.T,
         queries,

time: 69.1 us -> 66.6 us (0.964); the launches traced: 67.8 us -> 66.2 us
  Pallas kernels: 66.5 us -> 64.9 us
    pallas_call x1, Pallas kernels: 66.5 us -> 64.9 us  [split_shards(): pl.pallas_call(functools.partial(split_kernel, uly_count), out_shape=pltp...]
where the time goes in v4:
time: 66.6 us; the launch traced here: 66.2 us
  Pallas kernels  64.9 us (97%)
  local copies, waits for them, and re-layouts  1.32 us (2%)
    pallas_call x1, Pallas kernels, split_shards(): pl.pallas_call(functools.partial(split_kernel, uly_count), out_shape=pltp...  64.9 us

profile of v4, /device:TPU:0, one launch (start us, length us, event | category | flops | bytes accessed | tf_op | source)
XLA Modules:
  0.0 66.2 jit_solution(6581753680613494340)
XLA Ops:
  0.0 64.9 %split_and_attend.1 = bf16[128,8192]{1,0:T(8,128)(2,1)S(1)} custom-call(s32[6,64]{1,0:T(8,128)} %bitcast.2, s32[3,64]{1,0:T(4,128)} %bitcast.3, bf16[128,8192]{1,0:T(8,128)(2,1)} %q_hbm.1, bf16[128,1024]{1,0:T(8,128)(2,1)} %k_hbm.1, bf16[128,1024]{1,0:T(8,128)(2,1)} %v_hbm.1), custom_call_target="tpu_custom_call" | custom-call | tf_op jit(solution)/shard_map/split_and_attend/pallas_call | solution.py:660
  64.9 1.3 %copy.7 = bf16[128,8192]{1,0:T(8,128)(2,1)} copy(bf16[128,8192]{1,0:T(8,128)(2,1)S(1)} %split_and_attend.1) | data formatting | bytes 4194304

commit v5 on v4

--- a/solution.py
+++ b/solution.py
@@ -614,6 +614,7 @@
     tabulate(2)
     run(steps(1, 1) + steps(0, 3))
     ask(*PHASES[1])
+    ask(*PHASES[3])
     tabulate(3)
     run(steps(2, 0) + steps(1, 2) + steps(2, 1) + steps(1, 3))
     ask(*PHASES[2])
@@ -621,7 +622,7 @@
     between = (
         ((), (), steps(2, 2)[:1], steps(2, 2)[1:]),
         (steps(3, 1)[:1], steps(3, 1)[1:], steps(2, 3)[:1], steps(2, 3)[1:] + steps(3, 2)),
-        ((), steps(3, 3)[:1], steps(3, 3)[1:], ()),
+        (steps(3, 3)[:1], steps(3, 3)[1:], (), ()),
         ((), (), (), ()),
     )
     held_back = {0: (0,), 1: (1,), 2: (2,)}
@@ -632,8 +633,6 @@
             run(between[phase][gang])
             if phase == 3:
                 answer(phase, gang)
-        if phase == 1:
-            ask(*PHASES[3])
         for ready in held_back.get(phase, ()):
             for gang in range(gangs):
                 answer(ready, gang)

time: 66.6 us -> 66.3 us (level)
  the two profiles are of different devices: /device:TPU:0 before, /device:TPU:3 now
where the time goes in v5:
time: 66.3 us; the launch traced here: 66.2 us
  Pallas kernels  64.8 us (98%)
  local copies, waits for them, and re-layouts  1.32 us (2%)
    pallas_call x1, Pallas kernels, split_shards(): pl.pallas_call(functools.partial(split_kernel, uly_count), out_shape=pltp...  64.8 us

profile of v5, /device:TPU:3, one launch (start us, length us, event | category | flops | bytes accessed | tf_op | source)
XLA Modules:
  0.0 66.2 jit_solution(18003016374809535811)
XLA Ops:
  0.0 64.8 %split_and_attend.1 = bf16[128,8192]{1,0:T(8,128)(2,1)S(1)} custom-call(s32[6,64]{1,0:T(8,128)} %bitcast.2, s32[3,64]{1,0:T(4,128)} %bitcast.3, bf16[128,8192]{1,0:T(8,128)(2,1)} %q_hbm.1, bf16[128,1024]{1,0:T(8,128)(2,1)} %k_hbm.1, bf16[128,1024]{1,0:T(8,128)(2,1)} %v_hbm.1), custom_call_target="tpu_custom_call" | custom-call | tf_op jit(solution)/shard_map/split_and_attend/pallas_call | solution.py:659
  64.8 1.3 %copy.7 = bf16[128,8192]{1,0:T(8,128)(2,1)} copy(bf16[128,8192]{1,0:T(8,128)(2,1)S(1)} %split_and_attend.1) | data formatting | bytes 4194304

commit v6 on v5

--- a/solution.py
+++ b/solution.py
@@ -620,8 +620,8 @@
     ask(*PHASES[2])
     run(steps(3, 0))
     between = (
-        ((), (), steps(2, 2)[:1], steps(2, 2)[1:]),
-        (steps(3, 1)[:1], steps(3, 1)[1:], steps(2, 3)[:1], steps(2, 3)[1:] + steps(3, 2)),
+        ((), steps(2, 2)[:1], steps(2, 2)[1:], ()),
+        (steps(3, 1), steps(2, 3)[:1], steps(2, 3)[1:], steps(3, 2)),
         (steps(3, 3)[:1], steps(3, 3)[1:], (), ()),
         ((), (), (), ()),
     )

time: 66.3 us -> 66.2 us (level)
  the two profiles are of different devices: /device:TPU:3 before, /device:TPU:2 now
where the time goes in v6:
time: 66.2 us; the launch traced here: 66.1 us
  Pallas kernels  64.7 us (98%)
  local copies, waits for them, and re-layouts  1.32 us (2%)
    pallas_call x1, Pallas kernels, split_shards(): pl.pallas_call(functools.partial(split_kernel, uly_count), out_shape=pltp...  64.7 us

profile of v6, /device:TPU:2, one launch (start us, length us, event | category | flops | bytes accessed | tf_op | source)
XLA Modules:
  0.0 66.1 jit_solution(5983334507989756261)
XLA Ops:
  0.0 64.7 %split_and_attend.1 = bf16[128,8192]{1,0:T(8,128)(2,1)S(1)} custom-call(s32[6,64]{1,0:T(8,128)} %bitcast.2, s32[3,64]{1,0:T(4,128)} %bitcast.3, bf16[128,8192]{1,0:T(8,128)(2,1)} %q_hbm.1, bf16[128,1024]{1,0:T(8,128)(2,1)} %k_hbm.1, bf16[128,1024]{1,0:T(8,128)(2,1)} %v_hbm.1), custom_call_target="tpu_custom_call" | custom-call | tf_op jit(solution)/shard_map/split_and_attend/pallas_call | solution.py:659
  64.8 1.3 %copy.7 = bf16[128,8192]{1,0:T(8,128)(2,1)} copy(bf16[128,8192]{1,0:T(8,128)(2,1)S(1)} %split_and_attend.1) | data formatting | bytes 4194304
